TPU v7x, 256 devices: a whole 4x4x8 slice. The times are simulated.
256 devices in a mesh: row: 16 (over y_lo, z), col: 16 (over x, y_hi, core).
Axes of the slice: x: 4, y: 4 (y_hi: 2, y_lo: 2; y = y_hi * 2 + y_lo), z: 8, core: 2. Of those that a mesh axis runs over, the one named last changes fastest.
Arguments:
- residual: float32 [512, 512, 256], P('row', 'col'), may hold values from -6 to 6
- adjoint: float32 [512, 512, 256], P('row', 'col'), may hold values from -6 to 6
- coefficient: bfloat16 [512, 512, 256], P('row', 'col'), may hold values from 0.25 to 4
- basis_x: float32 [512, 512], replicated, may hold values from -0.25 to 0.25
- basis_y: float32 [512, 512], replicated, may hold values from -0.25 to 0.25
- basis_z: float32 [256, 256], replicated, may hold values from -0.375 to 0.375
- eigen_x: float32 [512], replicated, may hold values from 0.02 to 2
- eigen_y: float32 [512], replicated, may hold values from 0.02 to 2
- eigen_z: float32 [256], replicated, may hold values from 0.02 to 2
Outputs:
- adjoint_next: float32 [512, 512, 256], P('row', 'col')
- residual_next: float32 [512, 512, 256], P('row', 'col')
All inputs are finite; a program needn't handle non-finite values.
Results may differ from a plain program's by a relative error of at most 0.0003.
Values sent between devices are 32-bit elements; how exact they have to be, the bound alone decides.
A program may use at most 64 MiB of HBM per device.

v0:
```python
import jax
import jax.numpy as jnp
from jax import lax
from jax.sharding import PartitionSpec as P

MASS_TAPS = (
    1.0 / 5040,
    120.0 / 5040,
    1191.0 / 5040,
    2416.0 / 5040,
    1191.0 / 5040,
    120.0 / 5040,
    1.0 / 5040,
)
STIFF_TAPS = (-1.0 / 120, -0.2, -0.125, 2.0 / 3.0, -0.125, -0.2, -1.0 / 120)
HIGHEST = lax.Precision.HIGHEST


def with_halo(shard, sides, width):
    for axis, dim in sides:
        peers, length = (lax.axis_size(axis), shard.shape[dim])
        up = [(i, (i + 1) % peers) for i in range(peers - 1)]
        down = [(j, i) for i, j in up]
        last = lax.slice_in_dim(shard, length - width, length, axis=dim)
        leading = lax.slice_in_dim(shard, 0, width, axis=dim)
        before = lax.ppermute(last, axis, up)
        after = lax.ppermute(leading, axis, down)
        shard = jnp.concatenate([before, shard, after], axis=dim)
    return shard


def taps_along(padded, coeffs, axis_dim, length):
    running = coeffs[0] * lax.slice_in_dim(padded, 0, length, axis=axis_dim)
    for offset in range(1, 7):
        running = running + coeffs[offset] * lax.slice_in_dim(
            padded, offset, offset + length, axis=axis_dim
        )
    return running


def stiffness(padded, length_x, length_y, length_z):
    mass_x = taps_along(padded, MASS_TAPS, 0, length_x)
    stiff_x = taps_along(padded, STIFF_TAPS, 0, length_x)
    mass_xy = taps_along(mass_x, MASS_TAPS, 1, length_y)
    stiff_y = taps_along(mass_x, STIFF_TAPS, 1, length_y)
    stiff_xm = taps_along(stiff_x, MASS_TAPS, 1, length_y)
    return taps_along(stiff_y + stiff_xm, MASS_TAPS, 2, length_z) + taps_along(
        mass_xy, STIFF_TAPS, 2, length_z
    )


def shards(residual, adjoint, coefficient, basis_x, basis_y, basis_z, eigen_x, eigen_y, eigen_z):
    rows_local, cols_local, depth = residual.shape
    row_count = lax.axis_size("row")
    col_count = lax.axis_size("col")
    width_x = rows_local * row_count
    width_y = cols_local * col_count
    row_index = lax.axis_index("row")
    col_index = lax.axis_index("col")
    depth_part = depth // col_count
    ypart_row = width_y // row_count
    basis_zc = basis_z.reshape(depth, col_count, depth_part)
    basis_y4 = basis_y.reshape(col_count, cols_local, row_count, ypart_row)
    basis_x3 = basis_x.reshape(row_count, rows_local, width_x)
    outgoing = jnp.einsum("xyz,zjc->jcxy", residual, basis_zc, precision=HIGHEST)
    middle = jnp.einsum(
        "jcxy,jynr->ncxr",
        lax.all_to_all(outgoing, "col", split_axis=0, concat_axis=0, tiled=True),
        basis_y4,
        precision=HIGHEST,
    )
    spectrum = jnp.einsum(
        "icxr,ixk->crk",
        lax.all_to_all(middle, "row", split_axis=0, concat_axis=0, tiled=True),
        basis_x3,
        precision=HIGHEST,
    )
    zslice = lax.dynamic_slice_in_dim(eigen_z, col_index * depth_part, depth_part)
    yslice = lax.dynamic_slice_in_dim(eigen_y, row_index * ypart_row, ypart_row)
    denominator = zslice[:, None, None] + yslice[None, :, None] + eigen_x[None, None, :]
    scaled = spectrum / denominator
    returning = jnp.einsum("crk,ixk->icxr", scaled, basis_x3, precision=HIGHEST)
    middle_back = jnp.einsum(
        "ncxr,jynr->jcxy",
        lax.all_to_all(returning, "row", split_axis=0, concat_axis=0, tiled=True),
        basis_y4,
        precision=HIGHEST,
    )
    correction = jnp.einsum(
        "jcxy,zjc->xyz",
        lax.all_to_all(middle_back, "col", split_axis=0, concat_axis=0, tiled=True),
        basis_zc,
        precision=HIGHEST,
    )
    weighted = coefficient.astype(jnp.float32) * correction
    extended = with_halo(weighted, (("row", 0), ("col", 1)), 3)
    extended = jnp.pad(extended, ((0, 0), (0, 0), (3, 3)))
    image = stiffness(extended, rows_local, cols_local, depth)
    return (adjoint + correction, residual - image)


def solution(mesh):
    return jax.shard_map(
        shards,
        mesh=mesh,
        in_specs=(
            P("row", "col", None),
            P("row", "col", None),
            P("row", "col", None),
            P(),
            P(),
            P(),
            P(),
            P(),
            P(),
        ),
        out_specs=(P("row", "col", None), P("row", "col", None)),
        check_vma=False,
    )
```

profile of v0, /device:TPU:10, one launch (start us, length us, event | category | flops | bytes accessed | tf_op | source)
XLA Modules:
  0.0 316.4 jit_solution(14593513474820232902)
XLA Ops:
  0.6 1.2 copy.14
  1.8 6.0 %fusion.48 = f32[16,32,16,32]{3,2,1,0:T(8,128)} fusion(f32[256,16,16,1]{0,2,3,1:T(8,128)S(1)} %bitcast.87, f32[32,32,256]{2,1,0:T(8,128)} %param.9), kind=kOutput, calls=%fused_computation.82 | convolution fusion | flops 805306368 | bytes 2359296 | tf_op jit(solution)/shard_map/xyz,zjc->jcxy/dot_general | solution.py:65
  7.9 4.7 %reshape.63 = f32[16,1,16384]{2,1,0:T(1,128)} reshape(f32[16,32,16,32]{3,2,1,0:T(8,128)} %fusion.48) | data formatting | bytes 2097152
  12.6 7.0 %all-to-all-start = ((f32[16,1,16384]{2,1,0:T(1,128)}), f32[16,1,16384]{2,1,0:T(1,128)S(1)}, u32[]{:S(2)}, u32[]{:S(2)}) async-start(f32[16,1,16384]{2,1,0:T(1,128)} %reshape.63), calls=%async_computation | async-start | bytes 2097152 | tf_op jit(solution)/shard_map/all_to_all | solution.py:68
  19.6 2.5 reshape.47
  22.1 13.2 %all-to-all-done = f32[16,1,16384]{2,1,0:T(1,128)S(1)} async-done(((f32[16,1,16384]{2,1,0:T(1,128)}), f32[16,1,16384]{2,1,0:T(1,128)S(1)}, u32[]{:S(2)}, u32[]{:S(2)}) %all-to-all-start) | async-done | bytes 1048608 | tf_op jit(solution)/shard_map/all_to_all | solution.py:68
  35.3 0.5 broadcast.143
  35.8 3.1 reduce
  39.0 2.8 reshape.64
  41.8 2.8 bitcast_bitcast_fusion.1
  44.5 0.7 copy-done.2
  45.2 22.1 %fusion.8 = f32[16,16,32,32]{3,2,0,1:T(8,128)S(1)} fusion(f32[16,32,16,32]{3,2,1,0:T(8,128)S(1)} %copy-done.2, f32[16,16,32,32,1]{3,1,2,0,4:T(8,128)S(1)} %bitcast_bitcast_fusion.1), kind=kOutput, calls=%fused_computation.14 | convolution fusion | flops 1610612736 | bytes 3145728 | tf_op jit(solution)/shard_map/jcxy,jynr->ncxr/dot_general | solution.py:66
  67.3 2.6 copy.17
  69.9 4.7 %reshape.65 = f32[16,1,16384]{2,1,0:T(1,128)} reshape(f32[16,16,32,32]{3,2,1,0:T(8,128)} %copy.17) | data formatting | bytes 2097152
  74.6 10.6 %all-to-all-start.1 = ((f32[16,1,16384]{2,1,0:T(1,128)}), f32[16,1,16384]{2,1,0:T(1,128)S(1)}, u32[]{:S(2)}, u32[]{:S(2)}) async-start(f32[16,1,16384]{2,1,0:T(1,128)} %reshape.65), calls=%async_computation.1 | async-start | bytes 2097152 | tf_op jit(solution)/shard_map/all_to_all | solution.py:74
  85.2 0.8 dynamic_slice.7
  86.1 24.5 %all-to-all-done.1 = f32[16,1,16384]{2,1,0:T(1,128)S(1)} async-done(((f32[16,1,16384]{2,1,0:T(1,128)}), f32[16,1,16384]{2,1,0:T(1,128)S(1)}, u32[]{:S(2)}, u32[]{:S(2)}) %all-to-all-start.1) | async-done | bytes 1048608 | tf_op jit(solution)/shard_map/all_to_all | solution.py:74
  110.6 3.1 reduce.1
  113.8 2.8 reshape.66
  116.5 9.1 %convolution_bitcast_fusion.2 = f32[16,32,512]{2,1,0:T(8,128)S(1)} fusion(f32[16,16,32,32]{3,2,1,0:T(8,128)} %reshape.66, f32[16,32,512,1]{2,1,3,0:T(8,128)S(1)} %bitcast.83), kind=kOutput, calls=%fused_computation.35 | convolution fusion | flops 1610612736 | bytes 3145728 | tf_op jit(solution)/shard_map/icxr,ixk->crk/dot_general | solution.py:72
  125.6 6.8 %convolution_bitcast_fusion = f32[16,16,32,32]{2,3,0,1:T(8,128)S(1)} fusion(f32[16,32,512,1]{2,1,0,3:T(8,128)S(1)} %bitcast.82, f32[16,32,512]{2,1,0:T(8,128)S(1)} %convolution_bitcast_fusion.2, f32[512]{0:T(512)S(1)} %copy-done.8, f32[16,32]{1,0:T(8,128)S(1)} %broadcast_add_fusion), kind=kOutput, calls=%fused_computation.16 | convolution fusion | flops 1611137024 | bytes 3149824 | tf_op jit(solution)/shard_map/crk,ixk->icxr/dot_general | solution.py:82
  132.4 2.6 copy.72
  135.0 3.9 %reshape.67 = f32[16,1,16384]{2,1,0:T(1,128)S(1)} reshape(f32[16,16,32,32]{3,2,1,0:T(8,128)} %bitcast.84) | data formatting | bytes 2097152
  138.9 31.7 %all_to_all.20 = f32[16,1,16384]{2,1,0:T(1,128)S(1)} all-to-all(f32[16,1,16384]{2,1,0:T(1,128)S(1)} %reshape.67), channel_id=1, replica_groups=mesh['row'=16,'col'=16] {'row'}, dimensions={0} | all-to-all | bytes 2097152 | tf_op jit(solution)/shard_map/all_to_all | solution.py:85
  170.6 3.1 reduce.2
  173.7 2.8 reshape.68
  176.5 3.0 fusion.59
  179.5 0.5 copy-done.3
  179.9 52.9 %fusion.13 = f32[16,16,32,32]{3,2,0,1:T(8,128)S(1)} fusion(f32[16,32,16,32,1]{3,2,1,0,4:T(8,128)S(1)} %bitcast.86, f32[16,16,32,32,1]{2,3,0,4,1:T(8,128)S(1)} %fusion.59), kind=kOutput, calls=%fused_computation.15 | convolution fusion | flops 1610612736 | bytes 3145728 | tf_op jit(solution)/shard_map/ncxr,jynr->jcxy/dot_general | solution.py:83
  232.9 5.2 %copy.71 = f32[16,16,32,32]{3,1,2,0:T(8,128)} copy(f32[16,16,32,32]{3,2,0,1:T(8,128)S(1)} %fusion.13) | data formatting | bytes 2097152 | tf_op jit(solution)/shard_map/ncxr,jynr->jcxy/transpose | solution.py:83
  238.1 3.9 %reshape.69 = f32[16,1,16384]{2,1,0:T(1,128)S(1)} reshape(f32[16,32,16,32]{3,2,1,0:T(8,128)} %bitcast.85) | data formatting | bytes 2097152
  242.0 21.3 %all_to_all.21 = f32[16,1,16384]{2,1,0:T(1,128)S(1)} all-to-all(f32[16,1,16384]{2,1,0:T(1,128)S(1)} %reshape.69), channel_id=1, replica_groups=mesh['row'=16,'col'=16] {'col'}, dimensions={0} | all-to-all | bytes 2097152 | tf_op jit(solution)/shard_map/all_to_all | solution.py:91
  263.3 3.1 reduce.3
  266.5 2.7 reshape.70
  269.2 10.0 %convert_multiply_fusion = (f32[32,32,256]{2,1,0:T(8,128)S(1)}, f32[32,32,256]{2,1,0:T(8,128)}) fusion(bf16[32,32,256]{2,1,0:T(8,128)(2,1)S(1)} %copy-done.7, f32[32,32,256]{2,1,0:T(8,128)S(1)} %copy-done.6, f32[256,16,16,1]{0,2,3,1:T(8,128)S(1)} %bitcast.88, f32[16,32,16,32]{3,2,1,0:T(8,128)} %reshape.70), kind=kOutput, calls=%fused_computation.67 | convolution fusion | flops 806092800 | bytes 4980736 | tf_op jit(solution)/shard_map/jcxy,zjc->xyz/dot_general | solution.py:89
  279.2 5.4 %collective-permute-start.1 = (f32[3,32,256]{2,1,0:T(8,128)S(1)}, f32[3,32,256]{2,1,0:T(8,128)S(1)}, u32[]{:S(2)}, u32[]{:S(2)}) collective-permute-start(f32[3,32,256]{2,1,0:T(8,128)S(1)} %get-tuple-element.7), channel_id=1, source_target_pairs={{16,0},{32,16},{48,32},{64,48},{80,64},{96,80},{112,96},{128,112},... | collective-permute-start | bytes 294920 | tf_op jit(solution)/shard_map/ppermute | solution.py:27
  284.6 1.9 collective-permute-start
  286.6 0.4 collective-permute-done.1
  287.0 6.4 %collective-permute-done = f32[3,32,256]{2,1,0:T(8,128)S(1)} collective-permute-done((f32[3,32,256]{2,1,0:T(8,128)S(1)}, f32[3,32,256]{2,1,0:T(8,128)S(1)}, u32[]{:S(2)}, u32[]{:S(2)}) %collective-permute-start) | collective-permute-done | bytes 98336 | tf_op jit(solution)/shard_map/ppermute | solution.py:26
  293.4 2.4 collective-permute-start.3
  295.8 2.0 collective-permute-start.2
  297.8 0.8 collective-permute-done.3
  298.5 6.2 %collective-permute-done.2 = f32[38,3,256]{2,1,0:T(4,128)S(1)} collective-permute-done((f32[38,3,256]{2,1,0:T(4,128)S(1)}, f32[38,3,256]{2,1,0:T(4,128)S(1)}, u32[]{:S(2)}, u32[]{:S(2)}) %collective-permute-start.2) | collective-permute-done | bytes 116768 | tf_op jit(solution)/shard_map/ppermute | solution.py:26
  304.8 1.0 select_maximum_fusion
  305.8 2.2 multiply_add_fusion
  308.0 1.3 multiply_add_fusion.2
  309.3 2.6 fusion.19
  311.9 4.2 %fusion.27 = f32[32,32,256]{2,1,0:T(8,128)} fusion(f32[32,32,256]{2,1,0:T(8,128)S(1)} %copy-done.4, f32[32,32,262]{2,1,0:T(8,128)S(1)} %multiply_add_fusion.2, f32[32,32,262]{2,1,0:T(8,128)S(1)} %fusion.19), kind=kLoop, calls=%fused_computation.39 | loop fusion | flops 7340032 | bytes 16777216 | tf_op jit(solution)/shard_map/sub | solution.py:99
  (22 shorter events, 0.3 us)
Async XLA Ops:
  0.6 115.9 %copy-start = (f32[512,512]{1,0:T(8,128)S(1)}, f32[512,512]{1,0:T(8,128)}, u32[]{:S(2)}) copy-start(f32[512,512]{1,0:T(8,128)} %param.12) | copy-start | bytes 3145732
  12.6 7.0 %copy-start.5 = (f32[512,512]{1,0:T(8,128)S(1)}, f32[512,512]{1,0:T(8,128)}, u32[]{:S(2)}) copy-start(f32[512,512]{1,0:T(8,128)} %param.13) | copy-start | bytes 3145732
  12.6 22.8 %all-to-all-start = ((f32[16,1,16384]{2,1,0:T(1,128)}), f32[16,1,16384]{2,1,0:T(1,128)S(1)}, u32[]{:S(2)}, u32[]{:S(2)}) async-start(f32[16,1,16384]{2,1,0:T(1,128)} %reshape.63), calls=%async_computation | async-start | bytes 2097152 | tf_op jit(solution)/shard_map/all_to_all | solution.py:68
  41.8 3.4 %copy-start.2 = (f32[16,32,16,32]{3,2,1,0:T(8,128)S(1)}, f32[16,32,16,32]{3,2,1,0:T(8,128)}, u32[]{:S(2)}) copy-start(f32[16,32,16,32]{3,2,1,0:T(8,128)} %reshape.47) | copy-start | bytes 3145732
  74.6 11.3 %copy-start.9 = (f32[256]{0:T(256)S(1)}, f32[256]{0:T(256)}, u32[]{:S(2)}) copy-start(f32[256]{0:T(256)} %param.17) | copy-start | bytes 3076
  74.6 36.0 %all-to-all-start.1 = ((f32[16,1,16384]{2,1,0:T(1,128)}), f32[16,1,16384]{2,1,0:T(1,128)S(1)}, u32[]{:S(2)}, u32[]{:S(2)}) async-start(f32[16,1,16384]{2,1,0:T(1,128)} %reshape.65), calls=%async_computation.1 | async-start | bytes 2097152 | tf_op jit(solution)/shard_map/all_to_all | solution.py:74
  116.5 9.1 %copy-start.8 = (f32[512]{0:T(512)S(1)}, f32[512]{0:T(512)}, u32[]{:S(2)}) copy-start(f32[512]{0:T(512)} %param.15) | copy-start | bytes 6148
  176.5 3.4 %copy-start.3 = (f32[16,32,16,32]{3,2,1,0:T(8,128)S(1)}, f32[16,32,16,32]{3,2,1,0:T(8,128)}, u32[]{:S(2)}) copy-start(f32[16,32,16,32]{3,2,1,0:T(8,128)} %reshape.47) | copy-start | bytes 3145732
  266.5 2.8 copy-start.6
  266.5 2.7 copy-start.7
  279.2 7.8 %collective-permute-start.1 = (f32[3,32,256]{2,1,0:T(8,128)S(1)}, f32[3,32,256]{2,1,0:T(8,128)S(1)}, u32[]{:S(2)}, u32[]{:S(2)}) collective-permute-start(f32[3,32,256]{2,1,0:T(8,128)S(1)} %get-tuple-element.7), channel_id=1, source_target_pairs={{16,0},{32,16},{48,32},{64,48},{80,64},{96,80},{112,96},{128,112},... | collective-permute-start | bytes 294920 | tf_op jit(solution)/shard_map/ppermute | solution.py:27
  284.6 8.7 %collective-permute-start = (f32[3,32,256]{2,1,0:T(8,128)S(1)}, f32[3,32,256]{2,1,0:T(8,128)S(1)}, u32[]{:S(2)}, u32[]{:S(2)}) collective-permute-start(f32[3,32,256]{2,1,0:T(8,128)S(1)} %get-tuple-element.6), channel_id=1, source_target_pairs={{0,16},{16,32},{32,48},{48,64},{64,80},{80,96},{96,112},{112,128},... | collective-permute-start | bytes 294920 | tf_op jit(solution)/shard_map/ppermute | solution.py:26
  293.4 5.1 %collective-permute-start.3 = (f32[38,3,256]{2,1,0:T(4,128)S(1)}, f32[38,3,256]{2,1,0:T(4,128)S(1)}, u32[]{:S(2)}, u32[]{:S(2)}) collective-permute-start(f32[38,3,256]{2,1,0:T(4,128)S(1)} %get-tuple-element.5), channel_id=1, source_target_pairs={{1,0},{2,1},{3,2},{4,3},{5,4},{6,5},{7,6},{8,7},{9,8},{10,9},{11,1... | collective-permute-start | bytes 350216 | tf_op jit(solution)/shard_map/ppermute | solution.py:27
  295.8 9.0 %collective-permute-start.2 = (f32[38,3,256]{2,1,0:T(4,128)S(1)}, f32[38,3,256]{2,1,0:T(4,128)S(1)}, u32[]{:S(2)}, u32[]{:S(2)}) collective-permute-start(f32[38,3,256]{2,1,0:T(4,128)S(1)} %get-tuple-element.4), channel_id=1, source_target_pairs={{0,1},{1,2},{2,3},{3,4},{4,5},{5,6},{6,7},{7,8},{8,9},{9,10},{10,1... | collective-permute-start | bytes 350216 | tf_op jit(solution)/shard_map/ppermute | solution.py:26
  309.3 2.7 copy-start.4
  311.9 4.2 %copy-start.1 = (f32[512,512]{1,0:T(8,128)S(1)}, f32[512,512]{1,0:T(8,128)}, u32[]{:S(2)}) copy-start(f32[512,512]{1,0:T(8,128)} %param.12) | copy-start | bytes 3145732
where the time goes:
time: 320 us; the launch traced here: 316 us
  matrix products  107 us (33%)
  blocking collectives  53 us (17%)
  waiting for transfers between devices  51.5 us (16%)
  local copies, waits for them, and re-layouts  50.6 us (16%)
  starting transfers between devices  29.2 us (9%)
  other arithmetic  24.1 us (8%)
    dot_general x1, matrix products, shards(): jnp.einsum('ncxr,jynr->jcxy', lax.all_to_all(returning, 'row', split_axis...  52.9 us
    all_to_all x1, blocking collectives, shards(): lax.all_to_all(returning, 'row', split_axis=0, concat_axis=0, tiled=True)  31.7 us
    unnamed x29, local copies, waits for them, and re-layouts  30.5 us
    all_to_all x1, waiting for transfers between devices, shards(): lax.all_to_all(middle, 'row', split_axis=0, concat_axis=0, tiled=True)  24.5 us
    dot_general x1, matrix products, shards(): jnp.einsum('jcxy,jynr->ncxr', lax.all_to_all(outgoing, 'col', split_axis=...  22.1 us
    all_to_all x1, blocking collectives, shards(): lax.all_to_all(middle_back, 'col', split_axis=0, concat_axis=0, tiled=True)  21.3 us
    all_to_all x1, waiting for transfers between devices, shards(): lax.all_to_all(outgoing, 'col', split_axis=0, concat_axis=0, tiled=True)  13.2 us
    ppermute x2, waiting for transfers between devices, with_halo(): before = lax.ppermute(last, axis, up)  12.6 us
  transfers between devices with their start and end apart: 6, of which 6 were waited for; matrix products, arithmetic and copies ran while one was open for 1% of the time, Pallas kernels for 0%

commit v1 on v0

v1 whole, which is shorter than its diff:
```python
import jax
import jax.numpy as jnp
from jax import lax
from jax.experimental import pallas as pl
from jax.experimental.pallas import tpu as pltpu
from jax.sharding import PartitionSpec as P

MESH = pl.DeviceIdType.MESH
F32, BF16 = jnp.float32, jnp.bfloat16
N = 16
Q = 4
ROWS = 48
MASS = (2416.0, 1191.0, 120.0, 1.0)
STIFF = (80.0, -15.0, -24.0, -1.0)


def split(x):
    hi = x.astype(BF16)
    return hi, (x - hi.astype(F32)).astype(BF16)


def dot3(a, b, dims=((1,), (0,))):
    (ah, al), (bh, bl) = a, b

    def one(u, v):
        return lax.dot_general(u, v, (dims, ((), ())), preferred_element_type=F32)

    return one(ah, bh) + (one(ah, bl) + one(al, bh))


def transpose4(a):
    lane = lax.broadcasted_iota(jnp.int32, a[0].shape, 1)
    low, even = lane < 64, (lane & 32) == 0
    half = [pltpu.roll(v, 64, 1) for v in a]
    c = [
        jnp.where(low, a[0], half[2]),
        jnp.where(low, a[1], half[3]),
        jnp.where(low, half[0], a[2]),
        jnp.where(low, half[1], a[3]),
    ]
    return [
        jnp.where(even, c[0], pltpu.roll(c[1], 32, 1)),
        jnp.where(even, pltpu.roll(c[0], 96, 1), c[1]),
        jnp.where(even, c[2], pltpu.roll(c[3], 32, 1)),
        jnp.where(even, pltpu.roll(c[2], 96, 1), c[3]),
    ]


def taps(coeffs, scale, planes):
    total = (coeffs[0] * scale) * planes[0]
    for d in range(1, 4):
        total = total + (coeffs[d] * scale) * planes[d]
    return total


def band(coeffs, scale, n):
    i = lax.broadcasted_iota(jnp.int32, (n, n), 0)
    j = lax.broadcasted_iota(jnp.int32, (n, n), 1)
    dist = jnp.abs(i - j)
    total = jnp.zeros((n, n), F32)
    for d in range(4):
        total = jnp.where(dist == d, coeffs[d] * scale, total)
    return total


def kernel(
    res_ref, bz_ref, ex_ref, ey_ref, ez_ref, coef_any, bx_any, by_any,
    corr_ref, image_ref,
    coef, bx, by,
    lh, ll, lmh, lml, byh, byl, bxh, bxl, bxth, bxtl, zh, zl, ext, rowv,
    send_c, recv_c, send_r, recv_r, send_rb, recv_rb, send_cb, recv_cb,
    fbuf, ubuf, acc, wext, ypack, yrecv, corner, mixed,
    in_sem, send_sem, recv_sem, hsend_sem, hrecv_sem,
):
    r, n = lax.axis_index("row"), lax.axis_index("col")

    loads = [
        pltpu.make_async_copy(src, dst, in_sem.at[s])
        for s, (src, dst) in enumerate(((by_any, by), (bx_any, bx), (coef_any, coef)))
    ]
    for load in loads:
        load.start()

    barrier = pltpu.get_barrier_semaphore()

    def greet(d, _):
        pl.semaphore_signal(barrier, inc=1, device_id=(r, lax.rem(n + d, N)), device_id_type=MESH)
        pl.semaphore_signal(barrier, inc=1, device_id=(lax.rem(r + d, N), n), device_id_type=MESH)
        return 0

    lax.fori_loop(1, N, greet, 0)
    for dr in (1, N - 1):
        for dn in (1, N - 1):
            pl.semaphore_signal(
                barrier, inc=1, device_id=(lax.rem(r + dr, N), lax.rem(n + dn, N)), device_id_type=MESH
            )

    bzt = bz_ref[...].T
    top = lax.broadcasted_iota(jnp.int32, (8, 256), 0) < 4
    for p in range(32):
        v = bzt[8 * p : 8 * p + 8, :]
        w = pltpu.roll(v, 4, 0)
        for s, rows in enumerate((jnp.where(top, v, w), jnp.where(top, w, v))):
            at = pl.ds(16 * p + 8 * s, 8)
            fbuf[0, at, :] = rows[:, :128]
            fbuf[1, at, :] = rows[:, 128:]
    lmat = jnp.concatenate([fbuf[0], fbuf[1]], axis=1)
    lmat_h, lmat_l = split(lmat)
    lh[...] = lmat_h
    ll[...] = lmat_l

    def exchange(stage, k, src, dst, over_row):
        mine = r if over_row else n

        def one(d, _):
            peer = lax.rem(mine + d, N)
            pltpu.make_async_remote_copy(
                src_ref=src.at[k, peer],
                dst_ref=dst.at[k, mine],
                send_sem=send_sem.at[stage, k],
                recv_sem=recv_sem.at[stage, k],
                device_id=(peer, n) if over_row else (r, peer),
                device_id_type=MESH,
            ).start()
            return 0

        lax.fori_loop(1, N, one, 0)
        pltpu.make_async_copy(src.at[k, mine], dst.at[k, mine], recv_sem.at[stage, k]).start()

    def arrived(stage, k, dst):
        pltpu.make_async_copy(dst.at[k], dst.at[k], recv_sem.at[stage, k]).wait()

    data = [split(res_ref[16 * h : 16 * h + 16].reshape(512, 256)) for h in range(2)]
    top16 = lax.broadcasted_iota(jnp.int32, (N, 8, 512), 1) < 4
    for k in range(Q):
        rows = (lh[128 * k : 128 * k + 128, :], ll[128 * k : 128 * k + 128, :])
        a, b = (dot3(rows, data[h], ((1,), (1,))).reshape(N, 8, 512) for h in range(2))
        send_c[k] = jnp.where(top16, a, b)
        if k == 0:
            pl.semaphore_wait(barrier, 2 * (N - 1) + 4)
        exchange(0, k, send_c, recv_c, False)

    loads[0].wait()
    byh[...], byl[...] = split(by[...])
    loads[1].wait()
    bxh[...], bxl[...] = split(bx[...])
    bxth[...], bxtl[...] = split(bx[...].T)
    half0 = (lax.broadcasted_iota(jnp.int32, (512, 256), 0) & 4) == 0
    lm_h, lm_l = split(jnp.concatenate([jnp.where(half0, lmat, 0.0), jnp.where(half0, 0.0, lmat)], axis=1))
    lmh[...], lml[...] = lm_h, lm_l
    zh[:256, :], zl[:256, :] = split(band(MASS, 1.0 / 5040, 256))
    zh[256:, :], zl[256:, :] = split(band(STIFF, 1.0 / 120, 256))
    ext[...] = jnp.broadcast_to(ex_ref[...], (128, 512)).T
    lane = lax.broadcasted_iota(jnp.int32, (8, 128), 1)
    ey = pltpu.roll(jnp.broadcast_to(ey_ref[...], (8, 512)), lax.rem((N - r) * 32, 512), 1)[:, :128]
    ey = jnp.where(lane < 32, ey, 0.0)
    ey = ey + pltpu.roll(ey, 32, 1)
    ey = ey + pltpu.roll(ey, 64, 1)
    zlane = lax.broadcasted_iota(jnp.int32, (8, 256), 1)
    ez = jnp.broadcast_to(ez_ref[...], (8, 256))
    for k in range(Q):
        row = ey
        for c in range(4):
            one = jnp.sum(jnp.where(zlane == k * 64 + n * 4 + c, ez, 0.0), axis=1, keepdims=True)
            row = row + jnp.where((lane >= 32 * c) & (lane < 32 * c + 32), one, 0.0)
        rowv[k] = row

    def stage_y(k):
        arrived(0, k, recv_c)
        for g in range(4):
            for x in range(4):
                for t, v in enumerate(
                    transpose4([recv_c[k, 4 * g + m, :, 128 * x : 128 * x + 128] for m in range(4)])
                ):
                    fbuf[g, pl.ds(4 * x + t, 8, stride=16), :] = v
        f = jnp.concatenate([fbuf[g, :128, :] for g in range(4)], axis=1)
        s = dot3(split(f), (byh[...], byl[...]))
        for g in range(4):
            for x in range(2):
                blocks = [s[64 * x + 16 * c : 64 * x + 16 * c + 16, 128 * g : 128 * g + 128] for c in range(4)]
                for m, v in enumerate(transpose4(blocks)):
                    send_r[k, 4 * g + m, 16 * x : 16 * x + 16, :] = v
        exchange(1, k, send_r, recv_r, True)

    def stage_x(k):
        arrived(1, k, recv_r)
        spectrum = dot3((bxth[...], bxtl[...]), split(recv_r[k].reshape(512, 128)))
        scaled = spectrum / (ext[...] + rowv[k][:1, :])
        send_rb[k] = dot3((bxh[...], bxl[...]), split(scaled)).reshape(N, 32, 128)
        exchange(2, k, send_rb, recv_rb, True)

    def stage_yb(k):
        arrived(2, k, recv_rb)
        for g in range(4):
            for x in range(2):
                blocks = [recv_rb[k, 4 * g + m, 16 * x : 16 * x + 16, :] for m in range(4)]
                for c, v in enumerate(transpose4(blocks)):
                    ubuf[64 * x + 16 * c : 64 * x + 16 * c + 16, 128 * g : 128 * g + 128] = v
        p = dot3(split(ubuf[...]), (byh[...], byl[...]), ((1,), (1,)))
        for g in range(4):
            fbuf[g, :128, :] = p[:, 128 * g : 128 * g + 128]
        for g in range(4):
            for x in range(4):
                blocks = [fbuf[g, pl.ds(4 * x + t, 8, stride=16), :] for t in range(4)]
                for m, v in enumerate(transpose4(blocks)):
                    send_cb[k, 4 * g + m, :, 128 * x : 128 * x + 128] = v
        exchange(3, k, send_cb, recv_cb, False)

    def stage_zb(k):
        arrived(3, k, recv_cb)
        t = split(recv_cb[k].reshape(128, 512).T)
        rows = pl.ds(pl.multiple_of(128 * k, 128), 128)
        part = dot3(t, (lmh[rows, :], lml[rows, :]))
        for h in range(2):
            acc[512 * h : 512 * h + 512, :] = acc[512 * h : 512 * h + 512, :] + part[:, 256 * h : 256 * h + 256]

    acc[...] = jnp.zeros((1024, 256), F32)

    def step(s, _):
        @pl.when(s < Q)
        def _():
            stage_y(s)

        @pl.when((s >= 1) & (s < Q + 1))
        def _():
            stage_x(s - 1)

        @pl.when((s >= 3) & (s < Q + 3))
        def _():
            stage_yb(s - 3)

        @pl.when(s >= 5)
        def _():
            stage_zb(s - 5)

        return 0

    lax.fori_loop(0, Q + 5, step, 0)

    loads[2].wait()
    for x in range(32):
        c = acc[32 * x : 32 * x + 32, :]
        corr_ref[x] = c
        w = coef[x].astype(F32) * c
        at = pl.ds(ROWS * (x + 3) + 8, 32)
        wext[0, at, :] = w[:, :128]
        wext[1, at, :] = w[:, 128:]
    for side, first in ((0, 8), (1, 37)):
        for d in range(3):
            for h in range(2):
                ypack[side, d, h] = wext[h, pl.ds(3 * ROWS + first + d, 32, stride=ROWS), :]

    has = {(0, 0): None}
    for dr in (-1, 0, 1):
        for dn in (-1, 0, 1):
            ok_r = (r > 0) if dr < 0 else (r < N - 1)
            ok_n = (n > 0) if dn < 0 else (n < N - 1)
            has[dr, dn] = ok_n if dr == 0 else ok_r if dn == 0 else ok_r & ok_n

    def copies(dr, dn):
        peer = (r + dr, n + dn)
        out = []
        if dn == 0:
            for d in range(3):
                src = pl.ds(ROWS * ((3 if dr < 0 else 32) + d) + 8, 32)
                dst = pl.ds(ROWS * ((35 if dr < 0 else 0) + d) + 8, 32)
                out.append((wext.at[:, src, :], wext.at[:, dst, :], (0 if dr < 0 else 3) + d))
        elif dr == 0:
            side = 0 if dn < 0 else 1
            out.append((ypack.at[side], yrecv.at[1 - side], 6 + side))
        else:
            side = 0 if dn < 0 else 1
            which = 2 * (1 if dr < 0 else 0) + (1 - side)
            rows = pl.ds(0 if dr < 0 else 24, 8)
            out.append((ypack.at[side, :, :, rows, :], corner.at[which], 8 + which))
        return [
            pltpu.make_async_remote_copy(
                src_ref=a, dst_ref=b, send_sem=hsend_sem.at[s], recv_sem=hrecv_sem.at[s],
                device_id=peer, device_id_type=MESH,
            )
            for a, b, s in out
        ]

    sides = [(dr, dn) for dr in (-1, 0, 1) for dn in (-1, 0, 1) if (dr, dn) != (0, 0)]
    for dr, dn in sides:

        @pl.when(has[dr, dn])
        def _():
            for c in copies(dr, dn):
                c.start()

    for dr in (-1, 1):

        @pl.when(jnp.logical_not(has[dr, 0]))
        def _():
            for d in range(3):
                at = pl.ds(ROWS * ((0 if dr < 0 else 35) + d) + 8, 32)
                for h in range(2):
                    wext[h, at, :] = jnp.zeros((32, 128), F32)

    for dn in (-1, 1):

        @pl.when(jnp.logical_not(has[0, dn]))
        def _():
            yrecv[0 if dn < 0 else 1] = jnp.zeros((3, 2, 32, 128), F32)

        for dr in (-1, 1):

            @pl.when(jnp.logical_not(has[dr, dn]))
            def _():
                corner[2 * (0 if dr < 0 else 1) + (0 if dn < 0 else 1)] = jnp.zeros((3, 2, 8, 128), F32)

    for dr, dn in sides:

        @pl.when(has[dr, dn])
        def _():
            for c in copies(-dr, -dn):
                c.wait_recv()

    for side, first in ((0, 5), (1, 40)):
        for d in range(3):
            for h in range(2):
                wext[h, pl.ds(3 * ROWS + first + d, 32, stride=ROWS), :] = yrecv[side, d, h]
                for low_or_high, plane, row in ((0, 0, 5), (1, 35, 0)):
                    for i in range(3):
                        wext[h, pl.ds(ROWS * (plane + i) + first + d, 1), :] = corner[
                            2 * low_or_high + side, d, h, row + i : row + i + 1, :
                        ]

    def stencil(x, _):
        base = pl.multiple_of(x * ROWS, 8)
        for h in range(2):
            p = [wext[h, pl.ds(base + ROWS * i, ROWS), :] for i in range(7)]
            sums = [p[3], p[2] + p[4], p[1] + p[5], p[0] + p[6]]

            def along_y(v):
                return [v[8:40]] + [
                    pltpu.roll(v, d, 0)[8:40] + pltpu.roll(v, ROWS - d, 0)[8:40] for d in range(1, 4)
                ]

            mass = along_y(taps(MASS, 1.0 / 5040, sums))
            stiff = along_y(taps(STIFF, 1.0 / 120, sums))
            at = pl.ds(pl.multiple_of(x * 32, 32), 32)
            mixed[at, 128 * h : 128 * h + 128] = taps(STIFF, 1.0 / 120, mass) + taps(MASS, 1.0 / 5040, stiff)
            mixed[at, 256 + 128 * h : 256 + 128 * h + 128] = taps(MASS, 1.0 / 5040, mass)
        return 0

    lax.fori_loop(0, 32, stencil, 0)
    for i in range(4):
        m = split(mixed[256 * i : 256 * i + 256, :])
        image_ref[8 * i : 8 * i + 8] = dot3(m, (zh[...], zl[...])).reshape(8, 32, 256)

    for dr, dn in sides:

        @pl.when(has[dr, dn])
        def _():
            for c in copies(dr, dn):
                c.wait_send()

    for stage, src in enumerate((send_c, send_r, send_rb, send_cb)):
        for k in range(Q):
            sent = src.at[k, pl.ds(0, N - 1)]
            pltpu.make_async_copy(sent, sent, send_sem.at[stage, k]).wait()


def shards(residual, adjoint, coefficient, basis_x, basis_y, basis_z, eigen_x, eigen_y, eigen_z):
    field = jax.ShapeDtypeStruct((32, 32, 256), F32)
    vmem = pl.BlockSpec(memory_space=pltpu.VMEM)
    hbm = pl.BlockSpec(memory_space=pl.ANY)
    wide, tall = pltpu.VMEM((Q, N, 8, 512), F32), pltpu.VMEM((Q, N, 32, 128), F32)
    square = pltpu.VMEM((512, 512), BF16)
    correction, image = pl.pallas_call(
        kernel,
        out_shape=(field, field),
        in_specs=[vmem] * 5 + [hbm] * 3,
        out_specs=(vmem, vmem),
        scratch_shapes=[
            pltpu.VMEM((32, 32, 256), BF16),
            pltpu.VMEM((512, 512), F32),
            pltpu.VMEM((512, 512), F32),
            pltpu.VMEM((512, 256), BF16),
            pltpu.VMEM((512, 256), BF16),
            square, square, square, square, square, square, square, square,
            pltpu.VMEM((512, 256), BF16),
            pltpu.VMEM((512, 256), BF16),
            pltpu.VMEM((512, 128), F32),
            pltpu.VMEM((Q, 8, 128), F32),
            wide, wide, tall, tall, tall, tall, wide, wide,
            pltpu.VMEM((4, 512, 128), F32),
            pltpu.VMEM((128, 512), F32),
            pltpu.VMEM((1024, 256), F32),
            pltpu.VMEM((2, 38 * ROWS, 128), F32),
            pltpu.VMEM((2, 3, 2, 32, 128), F32),
            pltpu.VMEM((2, 3, 2, 32, 128), F32),
            pltpu.VMEM((4, 3, 2, 8, 128), F32),
            pltpu.VMEM((1024, 512), F32),
            pltpu.SemaphoreType.DMA((3,)),
            pltpu.SemaphoreType.DMA((4, Q)),
            pltpu.SemaphoreType.DMA((4, Q)),
            pltpu.SemaphoreType.DMA((12,)),
            pltpu.SemaphoreType.DMA((12,)),
        ],
        compiler_params=pltpu.CompilerParams(
            collective_id=0, has_side_effects=True, vmem_limit_bytes=56 * 1024 * 1024
        ),
    )(
        residual, basis_z, eigen_x.reshape(1, 512), eigen_y.reshape(1, 512), eigen_z.reshape(1, 256),
        coefficient, basis_x, basis_y,
    )
    return adjoint + correction, residual - image


def solution(mesh):
    field = P("row", "col", None)
    return jax.shard_map(
        shards,
        mesh=mesh,
        in_specs=(field, field, field, P(), P(), P(), P(), P(), P()),
        out_specs=(field, field),
        check_vma=False,
    )
```

time: 320 us -> 93.3 us (0.29)
  the two profiles are of different devices: /device:TPU:10 before, /device:TPU:1 now
where the time goes in v1:
time: 93.3 us; the launch traced here: 91.5 us
  Pallas kernels  87.2 us (93%)
  other arithmetic  3.66 us (4%)
    pallas_call x1, Pallas kernels, shards(): pl.pallas_call(kernel, out_shape=(field, field), in_specs=[vmem] * 5 + [h...  87.2 us
    add x1, other arithmetic, shards(): return (adjoint + correction, residual - image)  2.53 us

profile of v1, /device:TPU:1, one launch (start us, length us, event | category | flops | bytes accessed | tf_op | source)
XLA Modules:
  0.0 91.5 jit_solution(9486185250274207114)
XLA Ops:
  0.6 0.0 copy-start.1
  0.6 87.2 %shard_map.104 = (f32[32,32,256]{2,1,0:T(8,128)}, f32[32,32,256]{2,1,0:T(8,128)}) custom-call(f32[32,32,256]{2,1,0:T(8,128)} %res_ref.1, f32[256,256]{1,0:T(8,128)} %bz_ref.1, f32[1,512]{1,0:T(1,128)} %bitcast.3, f32[1,512]{1,0:T(1,128)} %bitcast.4, f32[1,256]{1,0:T(1,128)} %bitcast.5, bf16[32,32,256]{2,1,0:T(8,128)(2,1)} %coef_any.1, f32[512,512]{1,0:T(8,128)} %bx_any.1, ...), custom_call_target="tpu_custom_call" | custom-call | tf_op jit(solution)/shard_map/pallas_call | solution.py:372
  87.8 0.0 copy-done.1
  87.8 0.0 copy-start
  87.9 0.0 copy-start.2
  87.9 2.5 %add.3 = f32[32,32,256]{2,1,0:T(8,128)} add(f32[32,32,256]{2,1,0:T(8,128)S(1)} %copy-done.1, f32[32,32,256]{2,1,0:T(8,128)} %get-tuple-element.4) | non-fusion elementwise | flops 262144 | bytes 3145728 | tf_op jit(solution)/shard_map/add | solution.py:410
  90.4 0.0 copy-done
  90.4 0.0 copy-done.2
  90.4 1.1 %sub.3 = f32[32,32,256]{2,1,0:T(8,128)} subtract(f32[32,32,256]{2,1,0:T(8,128)S(1)} %copy-done, f32[32,32,256]{2,1,0:T(8,128)S(1)} %copy-done.2) | non-fusion elementwise | flops 262144 | bytes 3145728 | tf_op jit(solution)/shard_map/sub | solution.py:410
Async XLA Ops:
  0.6 87.2 %copy-start.1 = (f32[32,32,256]{2,1,0:T(8,128)S(1)}, f32[32,32,256]{2,1,0:T(8,128)}, u32[]{:S(2)}) copy-start(f32[32,32,256]{2,1,0:T(8,128)} %param.10) | copy-start | bytes 3145732
  87.8 2.6 %copy-start = (f32[32,32,256]{2,1,0:T(8,128)S(1)}, f32[32,32,256]{2,1,0:T(8,128)}, u32[]{:S(2)}) copy-start(f32[32,32,256]{2,1,0:T(8,128)} %res_ref.1) | copy-start | bytes 3145732
  87.9 2.5 %copy-start.2 = (f32[32,32,256]{2,1,0:T(8,128)S(1)}, f32[32,32,256]{2,1,0:T(8,128)}, u32[]{:S(2)}) copy-start(f32[32,32,256]{2,1,0:T(8,128)} %get-tuple-element.5) | copy-start | bytes 3145732

commit v2 on v1

--- a/solution.py
+++ b/solution.py
@@ -64,10 +64,10 @@
 
 
 def kernel(
-    res_ref, bz_ref, ex_ref, ey_ref, ez_ref, coef_any, bx_any, by_any,
+    bz_hbm, res_hbm, ex_hbm, ey_hbm, ez_hbm, bx_hbm, by_hbm, coef_hbm,
     corr_ref, image_ref,
-    coef, bx, by,
-    lh, ll, lmh, lml, byh, byl, bxh, bxl, bxth, bxtl, zh, zl, ext, rowv,
+    bz, res, ex, ey, ez, bx, by, coef, dh, dl,
+    lh, ll, lmh, lml, bh, bl, bth, btl, zh, zl, ext, rowv,
     send_c, recv_c, send_r, recv_r, send_rb, recv_rb, send_cb, recv_cb,
     fbuf, ubuf, acc, wext, ypack, yrecv, corner, mixed,
     in_sem, send_sem, recv_sem, hsend_sem, hrecv_sem,
@@ -76,7 +76,12 @@
 
     loads = [
         pltpu.make_async_copy(src, dst, in_sem.at[s])
-        for s, (src, dst) in enumerate(((by_any, by), (bx_any, bx), (coef_any, coef)))
+        for s, (src, dst) in enumerate(
+            (
+                (bz_hbm, bz), (res_hbm.at[:, :128], res.at[0]), (res_hbm.at[:, 128:], res.at[1]),
+                (bx_hbm, bx), (by_hbm, by), (ex_hbm, ex), (ey_hbm, ey), (ez_hbm, ez), (coef_hbm, coef),
+            )
+        )
     ]
     for load in loads:
         load.start()
@@ -95,7 +100,8 @@
                 barrier, inc=1, device_id=(lax.rem(r + dr, N), lax.rem(n + dn, N)), device_id_type=MESH
             )
 
-    bzt = bz_ref[...].T
+    loads[0].wait()
+    bzt = bz[...].T
     top = lax.broadcasted_iota(jnp.int32, (8, 256), 0) < 4
     for p in range(32):
         v = bzt[8 * p : 8 * p + 8, :]
@@ -113,7 +119,10 @@
         mine = r if over_row else n
 
         def one(d, _):
-            peer = lax.rem(mine + d, N)
+            if over_row:
+                peer = lax.rem(r // 8 + d // 8, 2) * 8 + lax.rem(r + d, 8)
+            else:
+                peer = lax.rem(n // 4 + d // 4, 4) * 4 + lax.rem(n // 2 + d // 2, 2) * 2 + lax.rem(n + d, 2)
             pltpu.make_async_remote_copy(
                 src_ref=src.at[k, peer],
                 dst_ref=dst.at[k, mine],
@@ -130,125 +139,133 @@
     def arrived(stage, k, dst):
         pltpu.make_async_copy(dst.at[k], dst.at[k], recv_sem.at[stage, k]).wait()
 
-    data = [split(res_ref[16 * h : 16 * h + 16].reshape(512, 256)) for h in range(2)]
+    loads[1].wait()
+    loads[2].wait()
     top16 = lax.broadcasted_iota(jnp.int32, (N, 8, 512), 1) < 4
-    for k in range(Q):
+
+    def stage_z(t, k):
         rows = (lh[128 * k : 128 * k + 128, :], ll[128 * k : 128 * k + 128, :])
-        a, b = (dot3(rows, data[h], ((1,), (1,))).reshape(N, 8, 512) for h in range(2))
-        send_c[k] = jnp.where(top16, a, b)
-        if k == 0:
-            pl.semaphore_wait(barrier, 2 * (N - 1) + 4)
-        exchange(0, k, send_c, recv_c, False)
-
-    loads[0].wait()
-    byh[...], byl[...] = split(by[...])
-    loads[1].wait()
-    bxh[...], bxl[...] = split(bx[...])
-    bxth[...], bxtl[...] = split(bx[...].T)
+        a, b = (
+            dot3(rows, (dh[t, 512 * h : 512 * h + 512, :], dl[t, 512 * h : 512 * h + 512, :]), ((1,), (1,)))
+            for h in range(2)
+        )
+        send_c[k] = jnp.where(top16, a.reshape(N, 8, 512), b.reshape(N, 8, 512))
+
+    for y in range(32):
+        plane = jnp.concatenate([res[h, pl.ds(y, 32, stride=32), :] for h in range(2)], axis=1)
+        dh[0, 32 * y : 32 * y + 32, :], dl[0, 32 * y : 32 * y + 32, :] = split(plane)
+    stage_z(0, 0)
+    pl.semaphore_wait(barrier, 2 * (N - 1) + 4)
+    exchange(0, 0, send_c, recv_c, True)
+    dh[1], dl[1] = split(jnp.concatenate([res[0], res[1]], axis=1))
+    stage_z(1, 2)
+    exchange(0, 2, send_c, recv_c, False)
+    stage_z(0, 1)
+    exchange(0, 1, send_c, recv_c, True)
+    stage_z(1, 3)
+    exchange(0, 3, send_c, recv_c, False)
+
+    loads[3].wait()
+    loads[4].wait()
+    for t, basis in enumerate((bx, by)):
+        bh[t], bl[t] = split(basis[...])
+        bth[t], btl[t] = split(basis[...].T)
     half0 = (lax.broadcasted_iota(jnp.int32, (512, 256), 0) & 4) == 0
-    lm_h, lm_l = split(jnp.concatenate([jnp.where(half0, lmat, 0.0), jnp.where(half0, 0.0, lmat)], axis=1))
-    lmh[...], lml[...] = lm_h, lm_l
+    lmh[...], lml[...] = split(jnp.concatenate([jnp.where(half0, lmat, 0.0), jnp.where(half0, 0.0, lmat)], axis=1))
     zh[:256, :], zl[:256, :] = split(band(MASS, 1.0 / 5040, 256))
     zh[256:, :], zl[256:, :] = split(band(STIFF, 1.0 / 120, 256))
-    ext[...] = jnp.broadcast_to(ex_ref[...], (128, 512)).T
+    for load in loads[5:8]:
+        load.wait()
     lane = lax.broadcasted_iota(jnp.int32, (8, 128), 1)
-    ey = pltpu.roll(jnp.broadcast_to(ey_ref[...], (8, 512)), lax.rem((N - r) * 32, 512), 1)[:, :128]
-    ey = jnp.where(lane < 32, ey, 0.0)
-    ey = ey + pltpu.roll(ey, 32, 1)
-    ey = ey + pltpu.roll(ey, 64, 1)
     zlane = lax.broadcasted_iota(jnp.int32, (8, 256), 1)
-    ez = jnp.broadcast_to(ez_ref[...], (8, 256))
-    for k in range(Q):
-        row = ey
-        for c in range(4):
-            one = jnp.sum(jnp.where(zlane == k * 64 + n * 4 + c, ez, 0.0), axis=1, keepdims=True)
-            row = row + jnp.where((lane >= 32 * c) & (lane < 32 * c + 32), one, 0.0)
-        rowv[k] = row
-
-    def stage_y(k):
+    ezs = jnp.broadcast_to(ez[...], (8, 256))
+    for t, (along, across, block, owner) in enumerate(((ey, ex, n, r), (ex, ey, r, n))):
+        ext[t] = jnp.broadcast_to(along[...], (128, 512)).T
+        own = pltpu.roll(jnp.broadcast_to(across[...], (8, 512)), lax.rem((N - block) * 32, 512), 1)[:, :128]
+        own = jnp.where(lane < 32, own, 0.0)
+        own = own + pltpu.roll(own, 32, 1)
+        own = own + pltpu.roll(own, 64, 1)
+        for k in (2 * t, 2 * t + 1):
+            row = own
+            for c in range(4):
+                one = jnp.sum(jnp.where(zlane == k * 64 + owner * 4 + c, ezs, 0.0), axis=1, keepdims=True)
+                row = row + jnp.where((lane >= 32 * c) & (lane < 32 * c + 32), one, 0.0)
+            rowv[k] = row
+
+    def first(t, k):
         arrived(0, k, recv_c)
         for g in range(4):
-            for x in range(4):
-                for t, v in enumerate(
-                    transpose4([recv_c[k, 4 * g + m, :, 128 * x : 128 * x + 128] for m in range(4)])
+            for y in range(4):
+                for u, v in enumerate(
+                    transpose4([recv_c[k, 4 * g + m, :, 128 * y : 128 * y + 128] for m in range(4)])
                 ):
-                    fbuf[g, pl.ds(4 * x + t, 8, stride=16), :] = v
+                    fbuf[g, pl.ds(4 * y + u, 8, stride=16), :] = v
         f = jnp.concatenate([fbuf[g, :128, :] for g in range(4)], axis=1)
-        s = dot3(split(f), (byh[...], byl[...]))
+        s = dot3(split(f), (bh[t], bl[t]))
         for g in range(4):
-            for x in range(2):
-                blocks = [s[64 * x + 16 * c : 64 * x + 16 * c + 16, 128 * g : 128 * g + 128] for c in range(4)]
+            for y in range(2):
+                blocks = [s[64 * y + 16 * c : 64 * y + 16 * c + 16, 128 * g : 128 * g + 128] for c in range(4)]
                 for m, v in enumerate(transpose4(blocks)):
-                    send_r[k, 4 * g + m, 16 * x : 16 * x + 16, :] = v
-        exchange(1, k, send_r, recv_r, True)
-
-    def stage_x(k):
+                    send_r[k, 4 * g + m, 16 * y : 16 * y + 16, :] = v
+        exchange(1, k, send_r, recv_r, t == 1)
+
+    def middle(t, k):
         arrived(1, k, recv_r)
-        spectrum = dot3((bxth[...], bxtl[...]), split(recv_r[k].reshape(512, 128)))
-        scaled = spectrum / (ext[...] + rowv[k][:1, :])
-        send_rb[k] = dot3((bxh[...], bxl[...]), split(scaled)).reshape(N, 32, 128)
-        exchange(2, k, send_rb, recv_rb, True)
-
-    def stage_yb(k):
+        spectrum = dot3((bth[1 - t], btl[1 - t]), split(recv_r[k].reshape(512, 128)))
+        scaled = spectrum / (ext[t] + rowv[k][:1, :])
+        send_rb[k] = dot3((bh[1 - t], bl[1 - t]), split(scaled)).reshape(N, 32, 128)
+        exchange(2, k, send_rb, recv_rb, t == 1)
+
+    def first_back(t, k):
         arrived(2, k, recv_rb)
         for g in range(4):
-            for x in range(2):
-                blocks = [recv_rb[k, 4 * g + m, 16 * x : 16 * x + 16, :] for m in range(4)]
+            for y in range(2):
+                blocks = [recv_rb[k, 4 * g + m, 16 * y : 16 * y + 16, :] for m in range(4)]
                 for c, v in enumerate(transpose4(blocks)):
-                    ubuf[64 * x + 16 * c : 64 * x + 16 * c + 16, 128 * g : 128 * g + 128] = v
-        p = dot3(split(ubuf[...]), (byh[...], byl[...]), ((1,), (1,)))
+                    ubuf[64 * y + 16 * c : 64 * y + 16 * c + 16, 128 * g : 128 * g + 128] = v
+        p = dot3(split(ubuf[...]), (bh[t], bl[t]), ((1,), (1,)))
         for g in range(4):
             fbuf[g, :128, :] = p[:, 128 * g : 128 * g + 128]
         for g in range(4):
-            for x in range(4):
-                blocks = [fbuf[g, pl.ds(4 * x + t, 8, stride=16), :] for t in range(4)]
+            for y in range(4):
+                blocks = [fbuf[g, pl.ds(4 * y + u, 8, stride=16), :] for u in range(4)]
                 for m, v in enumerate(transpose4(blocks)):
-                    send_cb[k, 4 * g + m, :, 128 * x : 128 * x + 128] = v
-        exchange(3, k, send_cb, recv_cb, False)
-
-    def stage_zb(k):
+                    send_cb[k, 4 * g + m, :, 128 * y : 128 * y + 128] = v
+        exchange(3, k, send_cb, recv_cb, t == 0)
+
+    def last(t, k):
         arrived(3, k, recv_cb)
-        t = split(recv_cb[k].reshape(128, 512).T)
+        data = split(recv_cb[k].reshape(128, 512).T)
         rows = pl.ds(pl.multiple_of(128 * k, 128), 128)
-        part = dot3(t, (lmh[rows, :], lml[rows, :]))
+        part = dot3(data, (lmh[rows, :], lml[rows, :]))
         for h in range(2):
-            acc[512 * h : 512 * h + 512, :] = acc[512 * h : 512 * h + 512, :] + part[:, 256 * h : 256 * h + 256]
-
-    acc[...] = jnp.zeros((1024, 256), F32)
-
-    def step(s, _):
-        @pl.when(s < Q)
-        def _():
-            stage_y(s)
-
-        @pl.when((s >= 1) & (s < Q + 1))
-        def _():
-            stage_x(s - 1)
-
-        @pl.when((s >= 3) & (s < Q + 3))
-        def _():
-            stage_yb(s - 3)
-
-        @pl.when(s >= 5)
-        def _():
-            stage_zb(s - 5)
-
-        return 0
-
-    lax.fori_loop(0, Q + 5, step, 0)
-
-    loads[2].wait()
-    for x in range(32):
-        c = acc[32 * x : 32 * x + 32, :]
-        corr_ref[x] = c
-        w = coef[x].astype(F32) * c
-        at = pl.ds(ROWS * (x + 3) + 8, 32)
-        wext[0, at, :] = w[:, :128]
-        wext[1, at, :] = w[:, 128:]
-    for side, first in ((0, 8), (1, 37)):
-        for d in range(3):
-            for h in range(2):
-                ypack[side, d, h] = wext[h, pl.ds(3 * ROWS + first + d, 32, stride=ROWS), :]
+            for w in range(2):
+                at = pl.ds(512 * h, 512)
+                acc[t, w, at, :] = acc[t, w, at, :] + part[:, 256 * h + 128 * w : 256 * h + 128 * w + 128]
+
+    acc[...] = jnp.zeros((2, 2, 1024, 128), F32)
+
+    def pairs(*steps):
+        def one(j, _):
+            for stage, t in steps:
+                stage(t, 2 * t + j)
+            return 0
+
+        lax.fori_loop(0, 2, one, 0)
+
+    pairs((first, 1), (first, 0))
+    pairs((middle, 0), (middle, 1))
+    pairs((first_back, 0))
+    pairs((first_back, 1))
+    pairs((last, 1), (last, 0))
+
+    loads[8].wait()
+
+    def weigh(x):
+        for h in range(2):
+            c = acc[0, h, pl.ds(x, 32, stride=32), :] + acc[1, h, 32 * x : 32 * x + 32, :]
+            corr_ref[x, :, 128 * h : 128 * h + 128] = c
+            wext[h, pl.ds(ROWS * (x + 3) + 8, 32), :] = coef[x, :, 128 * h : 128 * h + 128].astype(F32) * c
 
     has = {(0, 0): None}
     for dr in (-1, 0, 1):
@@ -282,12 +299,24 @@
         ]
 
     sides = [(dr, dn) for dr in (-1, 0, 1) for dn in (-1, 0, 1) if (dr, dn) != (0, 0)]
-    for dr, dn in sides:
-
-        @pl.when(has[dr, dn])
-        def _():
-            for c in copies(dr, dn):
-                c.start()
+    def send(some):
+        for dr, dn in some:
+
+            @pl.when(has[dr, dn])
+            def _():
+                for c in copies(dr, dn):
+                    c.start()
+
+    for x in (0, 1, 2, 29, 30, 31):
+        weigh(x)
+    send([d for d in sides if d[1] == 0])
+    for x in range(3, 29):
+        weigh(x)
+    for side, first in ((0, 8), (1, 37)):
+        for d in range(3):
+            for h in range(2):
+                ypack[side, d, h] = wext[h, pl.ds(3 * ROWS + first + d, 32, stride=ROWS), :]
+    send([d for d in sides if d[1] != 0])
 
     for dr in (-1, 1):
 
@@ -366,35 +395,42 @@
 def shards(residual, adjoint, coefficient, basis_x, basis_y, basis_z, eigen_x, eigen_y, eigen_z):
     field = jax.ShapeDtypeStruct((32, 32, 256), F32)
     vmem = pl.BlockSpec(memory_space=pltpu.VMEM)
-    hbm = pl.BlockSpec(memory_space=pl.ANY)
+    hbm = pl.BlockSpec(memory_space=pltpu.HBM)
     wide, tall = pltpu.VMEM((Q, N, 8, 512), F32), pltpu.VMEM((Q, N, 32, 128), F32)
-    square = pltpu.VMEM((512, 512), BF16)
+    square, pair = pltpu.VMEM((512, 512), BF16), pltpu.VMEM((2, 512, 512), BF16)
     correction, image = pl.pallas_call(
         kernel,
         out_shape=(field, field),
-        in_specs=[vmem] * 5 + [hbm] * 3,
+        in_specs=[hbm] * 8,
         out_specs=(vmem, vmem),
         scratch_shapes=[
-            pltpu.VMEM((32, 32, 256), BF16),
+            pltpu.VMEM((256, 256), F32),
+            pltpu.VMEM((2, 1024, 128), F32),
+            pltpu.VMEM((1, 512), F32),
+            pltpu.VMEM((1, 512), F32),
+            pltpu.VMEM((1, 256), F32),
             pltpu.VMEM((512, 512), F32),
             pltpu.VMEM((512, 512), F32),
+            pltpu.VMEM((32, 32, 256), BF16),
+            pltpu.VMEM((2, 1024, 256), BF16),
+            pltpu.VMEM((2, 1024, 256), BF16),
             pltpu.VMEM((512, 256), BF16),
             pltpu.VMEM((512, 256), BF16),
-            square, square, square, square, square, square, square, square,
+            square, square, pair, pair, pair, pair,
             pltpu.VMEM((512, 256), BF16),
             pltpu.VMEM((512, 256), BF16),
-            pltpu.VMEM((512, 128), F32),
+            pltpu.VMEM((2, 512, 128), F32),
             pltpu.VMEM((Q, 8, 128), F32),
             wide, wide, tall, tall, tall, tall, wide, wide,
             pltpu.VMEM((4, 512, 128), F32),
             pltpu.VMEM((128, 512), F32),
-            pltpu.VMEM((1024, 256), F32),
+            pltpu.VMEM((2, 2, 1024, 128), F32),
             pltpu.VMEM((2, 38 * ROWS, 128), F32),
             pltpu.VMEM((2, 3, 2, 32, 128), F32),
             pltpu.VMEM((2, 3, 2, 32, 128), F32),
             pltpu.VMEM((4, 3, 2, 8, 128), F32),
             pltpu.VMEM((1024, 512), F32),
-            pltpu.SemaphoreType.DMA((3,)),
+            pltpu.SemaphoreType.DMA((9,)),
             pltpu.SemaphoreType.DMA((4, Q)),
             pltpu.SemaphoreType.DMA((4, Q)),
             pltpu.SemaphoreType.DMA((12,)),
@@ -404,8 +440,9 @@
             collective_id=0, has_side_effects=True, vmem_limit_bytes=56 * 1024 * 1024
         ),
     )(
-        residual, basis_z, eigen_x.reshape(1, 512), eigen_y.reshape(1, 512), eigen_z.reshape(1, 256),
-        coefficient, basis_x, basis_y,
+        basis_z, residual.reshape(1024, 256),
+        eigen_x.reshape(1, 512), eigen_y.reshape(1, 512), eigen_z.reshape(1, 256),
+        basis_x, basis_y, coefficient,
     )
     return adjoint + correction, residual - image
 

time: 93.3 us -> 83.6 us (0.90); the launches traced: 91.5 us -> 83.5 us
  Pallas kernels: 87.2 us -> 79.2 us
    pallas_call x1, Pallas kernels: 87.2 us -> 79.2 us  [shards(): pl.pallas_call(kernel, out_shape=(field, field), in_specs=[hbm] * 8, out_...]
where the time goes in v2:
time: 83.6 us; the launch traced here: 83.5 us
  Pallas kernels  79.2 us (95%)
  other arithmetic  3.66 us (4%)
    pallas_call x1, Pallas kernels, shards(): pl.pallas_call(kernel, out_shape=(field, field), in_specs=[hbm] * 8, out_...  79.2 us
    add x1, other arithmetic, shards(): return (adjoint + correction, residual - image)  2.53 us

profile of v2, /device:TPU:1, one launch (start us, length us, event | category | flops | bytes accessed | tf_op | source)
XLA Modules:
  0.0 83.5 jit_solution(12527330612028879927)
XLA Ops:
  0.6 0.0 copy-start.1
  0.6 79.2 %shard_map.104 = (f32[32,32,256]{2,1,0:T(8,128)}, f32[32,32,256]{2,1,0:T(8,128)}) custom-call(f32[256,256]{1,0:T(8,128)} %bz_hbm.1, f32[1024,256]{1,0:T(8,128)} %bitcast.4, f32[1,512]{1,0:T(1,128)} %bitcast.5, f32[1,512]{1,0:T(1,128)} %bitcast.6, f32[1,256]{1,0:T(1,128)} %bitcast.7, f32[512,512]{1,0:T(8,128)} %bx_hbm.1, f32[512,512]{1,0:T(8,128)} %by_hbm.1, ...), custom_call_target="tpu_custom_call" | custom-call | tf_op jit(solution)/shard_map/pallas_call | solution.py:401
  79.8 0.0 copy-done.1
  79.8 0.0 copy-start
  79.9 0.0 copy-start.2
  79.9 2.5 %add.3 = f32[32,32,256]{2,1,0:T(8,128)} add(f32[32,32,256]{2,1,0:T(8,128)S(1)} %copy-done.1, f32[32,32,256]{2,1,0:T(8,128)} %get-tuple-element.4) | non-fusion elementwise | flops 262144 | bytes 3145728 | tf_op jit(solution)/shard_map/add | solution.py:447
  82.4 0.0 copy-done
  82.4 0.0 copy-done.2
  82.4 1.1 %sub.3 = f32[32,32,256]{2,1,0:T(8,128)} subtract(f32[32,32,256]{2,1,0:T(8,128)S(1)} %copy-done, f32[32,32,256]{2,1,0:T(8,128)S(1)} %copy-done.2) | non-fusion elementwise | flops 262144 | bytes 3145728 | tf_op jit(solution)/shard_map/sub | solution.py:447
Async XLA Ops:
  0.6 79.2 %copy-start.1 = (f32[32,32,256]{2,1,0:T(8,128)S(1)}, f32[32,32,256]{2,1,0:T(8,128)}, u32[]{:S(2)}) copy-start(f32[32,32,256]{2,1,0:T(8,128)} %param.10) | copy-start | bytes 3145732
  79.8 2.6 %copy-start = (f32[32,32,256]{2,1,0:T(8,128)S(1)}, f32[32,32,256]{2,1,0:T(8,128)}, u32[]{:S(2)}) copy-start(f32[32,32,256]{2,1,0:T(8,128)} %param.9) | copy-start | bytes 3145732
  79.9 2.5 %copy-start.2 = (f32[32,32,256]{2,1,0:T(8,128)S(1)}, f32[32,32,256]{2,1,0:T(8,128)}, u32[]{:S(2)}) copy-start(f32[32,32,256]{2,1,0:T(8,128)} %get-tuple-element.5) | copy-start | bytes 3145732

commit v3 on v2

--- a/solution.py
+++ b/solution.py
@@ -64,13 +64,13 @@
 
 
 def kernel(
-    bz_hbm, res_hbm, ex_hbm, ey_hbm, ez_hbm, bx_hbm, by_hbm, coef_hbm,
-    corr_ref, image_ref,
-    bz, res, ex, ey, ez, bx, by, coef, dh, dl,
+    bz_hbm, res_hbm, ex_hbm, ey_hbm, ez_hbm, bx_hbm, by_hbm, coef_hbm, adj_hbm,
+    adj_out, res_out,
+    bz, res, ex, ey, ez, bx, by, coef, adj, dh, dl,
     lh, ll, lmh, lml, bh, bl, bth, btl, zh, zl, ext, rowv,
     send_c, recv_c, send_r, recv_r, send_rb, recv_rb, send_cb, recv_cb,
-    fbuf, ubuf, acc, wext, ypack, yrecv, corner, mixed,
-    in_sem, send_sem, recv_sem, hsend_sem, hrecv_sem,
+    fbuf, ubuf, acc, wext, ypack, hext, mixed,
+    in_sem, out_sem, send_sem, recv_sem, hsend_sem, hrecv_sem,
 ):
     r, n = lax.axis_index("row"), lax.axis_index("col")
 
@@ -80,6 +80,7 @@
             (
                 (bz_hbm, bz), (res_hbm.at[:, :128], res.at[0]), (res_hbm.at[:, 128:], res.at[1]),
                 (bx_hbm, bx), (by_hbm, by), (ex_hbm, ex), (ey_hbm, ey), (ez_hbm, ez), (coef_hbm, coef),
+                (adj_hbm, adj),
             )
         )
     ]
@@ -101,19 +102,21 @@
             )
 
     loads[0].wait()
-    bzt = bz[...].T
     top = lax.broadcasted_iota(jnp.int32, (8, 256), 0) < 4
-    for p in range(32):
-        v = bzt[8 * p : 8 * p + 8, :]
-        w = pltpu.roll(v, 4, 0)
-        for s, rows in enumerate((jnp.where(top, v, w), jnp.where(top, w, v))):
-            at = pl.ds(16 * p + 8 * s, 8)
-            fbuf[0, at, :] = rows[:, :128]
-            fbuf[1, at, :] = rows[:, 128:]
-    lmat = jnp.concatenate([fbuf[0], fbuf[1]], axis=1)
-    lmat_h, lmat_l = split(lmat)
-    lh[...] = lmat_h
-    ll[...] = lmat_l
+
+    def prepare(t):
+        bzt = bz[:, 128 * t : 128 * t + 128].T
+        for p in range(16):
+            v = bzt[8 * p : 8 * p + 8, :]
+            w = pltpu.roll(v, 4, 0)
+            for i, rows in enumerate((jnp.where(top, v, w), jnp.where(top, w, v))):
+                at = pl.ds(256 * t + 16 * p + 8 * i, 8)
+                fbuf[0, at, :] = rows[:, :128]
+                fbuf[1, at, :] = rows[:, 128:]
+        at = pl.ds(256 * t, 256)
+        lh[at, :], ll[at, :] = split(jnp.concatenate([fbuf[0, at, :], fbuf[1, at, :]], axis=1))
+
+    prepare(0)
 
     def exchange(stage, k, src, dst, over_row):
         mine = r if over_row else n
@@ -157,6 +160,7 @@
     stage_z(0, 0)
     pl.semaphore_wait(barrier, 2 * (N - 1) + 4)
     exchange(0, 0, send_c, recv_c, True)
+    prepare(1)
     dh[1], dl[1] = split(jnp.concatenate([res[0], res[1]], axis=1))
     stage_z(1, 2)
     exchange(0, 2, send_c, recv_c, False)
@@ -170,6 +174,7 @@
     for t, basis in enumerate((bx, by)):
         bh[t], bl[t] = split(basis[...])
         bth[t], btl[t] = split(basis[...].T)
+    lmat = jnp.concatenate([fbuf[0], fbuf[1]], axis=1)
     half0 = (lax.broadcasted_iota(jnp.int32, (512, 256), 0) & 4) == 0
     lmh[...], lml[...] = split(jnp.concatenate([jnp.where(half0, lmat, 0.0), jnp.where(half0, 0.0, lmat)], axis=1))
     zh[:256, :], zl[:256, :] = split(band(MASS, 1.0 / 5040, 256))
@@ -244,6 +249,10 @@
                 acc[t, w, at, :] = acc[t, w, at, :] + part[:, 256 * h + 128 * w : 256 * h + 128 * w + 128]
 
     acc[...] = jnp.zeros((2, 2, 1024, 128), F32)
+    for x in range(38):
+        for h in range(2):
+            wext[h, ROWS * x : ROWS * x + 8, :] = jnp.zeros((8, 128), F32)
+            wext[h, ROWS * x + 40 : ROWS * x + 48, :] = jnp.zeros((8, 128), F32)
 
     def pairs(*steps):
         def one(j, _):
@@ -264,7 +273,6 @@
     def weigh(x):
         for h in range(2):
             c = acc[0, h, pl.ds(x, 32, stride=32), :] + acc[1, h, 32 * x : 32 * x + 32, :]
-            corr_ref[x, :, 128 * h : 128 * h + 128] = c
             wext[h, pl.ds(ROWS * (x + 3) + 8, 32), :] = coef[x, :, 128 * h : 128 * h + 128].astype(F32) * c
 
     has = {(0, 0): None}
@@ -284,12 +292,17 @@
                 out.append((wext.at[:, src, :], wext.at[:, dst, :], (0 if dr < 0 else 3) + d))
         elif dr == 0:
             side = 0 if dn < 0 else 1
-            out.append((ypack.at[side], yrecv.at[1 - side], 6 + side))
+            out.append((ypack.at[side], hext.at[1 - side, :, :, pl.ds(8, 32), :], 6 + side))
         else:
             side = 0 if dn < 0 else 1
-            which = 2 * (1 if dr < 0 else 0) + (1 - side)
-            rows = pl.ds(0 if dr < 0 else 24, 8)
-            out.append((ypack.at[side, :, :, rows, :], corner.at[which], 8 + which))
+            rows, at = (0, 40) if dr < 0 else (24, 0)
+            out.append(
+                (
+                    ypack.at[side, :, :, pl.ds(rows, 8), :],
+                    hext.at[1 - side, :, :, pl.ds(at, 8), :],
+                    8 + 2 * (dr > 0) + side,
+                )
+            )
         return [
             pltpu.make_async_remote_copy(
                 src_ref=a, dst_ref=b, send_sem=hsend_sem.at[s], recv_sem=hrecv_sem.at[s],
@@ -307,16 +320,14 @@
                 for c in copies(dr, dn):
                     c.start()
 
-    for x in (0, 1, 2, 29, 30, 31):
-        weigh(x)
-    send([d for d in sides if d[1] == 0])
-    for x in range(3, 29):
+    for x in range(32):
         weigh(x)
     for side, first in ((0, 8), (1, 37)):
         for d in range(3):
             for h in range(2):
                 ypack[side, d, h] = wext[h, pl.ds(3 * ROWS + first + d, 32, stride=ROWS), :]
-    send([d for d in sides if d[1] != 0])
+    send([d for d in sides if d[0] == 0])
+    send([d for d in sides if d[0] != 0])
 
     for dr in (-1, 1):
 
@@ -331,30 +342,36 @@
 
         @pl.when(jnp.logical_not(has[0, dn]))
         def _():
-            yrecv[0 if dn < 0 else 1] = jnp.zeros((3, 2, 32, 128), F32)
+            hext[0 if dn < 0 else 1, :, :, 8:40, :] = jnp.zeros((3, 2, 32, 128), F32)
 
         for dr in (-1, 1):
 
             @pl.when(jnp.logical_not(has[dr, dn]))
             def _():
-                corner[2 * (0 if dr < 0 else 1) + (0 if dn < 0 else 1)] = jnp.zeros((3, 2, 8, 128), F32)
-
-    for dr, dn in sides:
-
-        @pl.when(has[dr, dn])
-        def _():
-            for c in copies(-dr, -dn):
-                c.wait_recv()
-
-    for side, first in ((0, 5), (1, 40)):
-        for d in range(3):
-            for h in range(2):
-                wext[h, pl.ds(3 * ROWS + first + d, 32, stride=ROWS), :] = yrecv[side, d, h]
-                for low_or_high, plane, row in ((0, 0, 5), (1, 35, 0)):
-                    for i in range(3):
-                        wext[h, pl.ds(ROWS * (plane + i) + first + d, 1), :] = corner[
-                            2 * low_or_high + side, d, h, row + i : row + i + 1, :
-                        ]
+                at = 0 if dr < 0 else 40
+                hext[0 if dn < 0 else 1, :, :, at : at + 8, :] = jnp.zeros((3, 2, 8, 128), F32)
+
+    loads[9].wait()
+    for x in range(32):
+        for h in range(2):
+            c = acc[0, h, pl.ds(x, 32, stride=32), :] + acc[1, h, 32 * x : 32 * x + 32, :]
+            at = slice(128 * h, 128 * h + 128)
+            adj[32 * x : 32 * x + 32, at] = adj[32 * x : 32 * x + 32, at] + c
+    stores = [pltpu.make_async_copy(adj, adj_out, out_sem.at[0])]
+    stores[0].start()
+
+    def receive(some):
+        for dr, dn in some:
+
+            @pl.when(has[dr, dn])
+            def _():
+                for c in copies(-dr, -dn):
+                    c.wait_recv()
+
+    receive([d for d in sides if d[1] == 0])
+
+    def along_rows(v):
+        return [v[8:40]] + [pltpu.roll(v, d, 0)[8:40] + pltpu.roll(v, ROWS - d, 0)[8:40] for d in range(1, 4)]
 
     def stencil(x, _):
         base = pl.multiple_of(x * ROWS, 8)
@@ -362,13 +379,8 @@
             p = [wext[h, pl.ds(base + ROWS * i, ROWS), :] for i in range(7)]
             sums = [p[3], p[2] + p[4], p[1] + p[5], p[0] + p[6]]
 
-            def along_y(v):
-                return [v[8:40]] + [
-                    pltpu.roll(v, d, 0)[8:40] + pltpu.roll(v, ROWS - d, 0)[8:40] for d in range(1, 4)
-                ]
-
-            mass = along_y(taps(MASS, 1.0 / 5040, sums))
-            stiff = along_y(taps(STIFF, 1.0 / 120, sums))
+            mass = along_rows(taps(MASS, 1.0 / 5040, sums))
+            stiff = along_rows(taps(STIFF, 1.0 / 120, sums))
             at = pl.ds(pl.multiple_of(x * 32, 32), 32)
             mixed[at, 128 * h : 128 * h + 128] = taps(STIFF, 1.0 / 120, mass) + taps(MASS, 1.0 / 5040, stiff)
             mixed[at, 256 + 128 * h : 256 + 128 * h + 128] = taps(MASS, 1.0 / 5040, mass)
@@ -376,8 +388,36 @@
 
     lax.fori_loop(0, 32, stencil, 0)
     for i in range(4):
-        m = split(mixed[256 * i : 256 * i + 256, :])
-        image_ref[8 * i : 8 * i + 8] = dot3(m, (zh[...], zl[...])).reshape(8, 32, 256)
+        at = slice(256 * i, 256 * i + 256)
+        image = dot3(split(mixed[at, :]), (zh[...], zl[...]))
+        for h in range(2):
+            res[h, at, :] = res[h, at, :] - image[:, 128 * h : 128 * h + 128]
+
+    receive([d for d in sides if d[1] != 0])
+    for side in range(2):
+        for h in range(2):
+            near = [along_rows(hext[side, d, h]) for d in range(3)]
+            mass = [taps(MASS, 1.0 / 5040, v) for v in near]
+            stiff = [taps(STIFF, 1.0 / 120, v) for v in near]
+            for o in range(3):
+                a = b = jnp.zeros((32, 128), F32)
+                for d in range(o, 3) if side == 0 else range(o + 1):
+                    dist = o + 3 - d if side == 0 else 3 + d - o
+                    a = a + (STIFF[dist] / 120) * mass[d] + (MASS[dist] / 5040) * stiff[d]
+                    b = b + (MASS[dist] / 5040) * mass[d]
+                at = slice(96 * side + 32 * o, 96 * side + 32 * o + 32)
+                mixed[at, 128 * h : 128 * h + 128] = a
+                mixed[at, 256 + 128 * h : 256 + 128 * h + 128] = b
+    image = dot3(split(mixed[:192, :]), (zh[...], zl[...]))
+    for h in range(2):
+        for side in range(2):
+            for o in range(3):
+                at = pl.ds(o if side == 0 else 29 + o, 32, stride=32)
+                part = image[96 * side + 32 * o : 96 * side + 32 * o + 32, 128 * h : 128 * h + 128]
+                res[h, at, :] = res[h, at, :] - part
+        store = pltpu.make_async_copy(res.at[h], res_out.at[:, pl.ds(128 * h, 128)], out_sem.at[1 + h])
+        store.start()
+        stores.append(store)
 
     for dr, dn in sides:
 
@@ -391,18 +431,20 @@
             sent = src.at[k, pl.ds(0, N - 1)]
             pltpu.make_async_copy(sent, sent, send_sem.at[stage, k]).wait()
 
+    for store in stores:
+        store.wait()
+
 
 def shards(residual, adjoint, coefficient, basis_x, basis_y, basis_z, eigen_x, eigen_y, eigen_z):
-    field = jax.ShapeDtypeStruct((32, 32, 256), F32)
-    vmem = pl.BlockSpec(memory_space=pltpu.VMEM)
+    field = jax.ShapeDtypeStruct((1024, 256), F32)
     hbm = pl.BlockSpec(memory_space=pltpu.HBM)
     wide, tall = pltpu.VMEM((Q, N, 8, 512), F32), pltpu.VMEM((Q, N, 32, 128), F32)
     square, pair = pltpu.VMEM((512, 512), BF16), pltpu.VMEM((2, 512, 512), BF16)
-    correction, image = pl.pallas_call(
+    adjoint_next, residual_next = pl.pallas_call(
         kernel,
         out_shape=(field, field),
-        in_specs=[hbm] * 8,
-        out_specs=(vmem, vmem),
+        in_specs=[hbm] * 9,
+        out_specs=(hbm, hbm),
         scratch_shapes=[
             pltpu.VMEM((256, 256), F32),
             pltpu.VMEM((2, 1024, 128), F32),
@@ -412,6 +454,7 @@
             pltpu.VMEM((512, 512), F32),
             pltpu.VMEM((512, 512), F32),
             pltpu.VMEM((32, 32, 256), BF16),
+            pltpu.VMEM((1024, 256), F32),
             pltpu.VMEM((2, 1024, 256), BF16),
             pltpu.VMEM((2, 1024, 256), BF16),
             pltpu.VMEM((512, 256), BF16),
@@ -427,10 +470,10 @@
             pltpu.VMEM((2, 2, 1024, 128), F32),
             pltpu.VMEM((2, 38 * ROWS, 128), F32),
             pltpu.VMEM((2, 3, 2, 32, 128), F32),
-            pltpu.VMEM((2, 3, 2, 32, 128), F32),
-            pltpu.VMEM((4, 3, 2, 8, 128), F32),
+            pltpu.VMEM((2, 3, 2, ROWS, 128), F32),
             pltpu.VMEM((1024, 512), F32),
-            pltpu.SemaphoreType.DMA((9,)),
+            pltpu.SemaphoreType.DMA((10,)),
+            pltpu.SemaphoreType.DMA((3,)),
             pltpu.SemaphoreType.DMA((4, Q)),
             pltpu.SemaphoreType.DMA((4, Q)),
             pltpu.SemaphoreType.DMA((12,)),
@@ -442,9 +485,9 @@
     )(
         basis_z, residual.reshape(1024, 256),
         eigen_x.reshape(1, 512), eigen_y.reshape(1, 512), eigen_z.reshape(1, 256),
-        basis_x, basis_y, coefficient,
+        basis_x, basis_y, coefficient, adjoint.reshape(1024, 256),
     )
-    return adjoint + correction, residual - image
+    return adjoint_next.reshape(32, 32, 256), residual_next.reshape(32, 32, 256)
 
 
 def solution(mesh):

time: 83.6 us -> 80.5 us (0.963)
  other arithmetic: 3.66 us -> 0 us
  local copies, waits for them, and re-layouts: 0.01 us -> 3.37 us
  Pallas kernels: 79.2 us -> 76.4 us
    unnamed x6 -> x4, local copies, waits for them, and re-layouts: 0.01 us -> 3.37 us
    pallas_call x1, Pallas kernels: 79.2 us -> 76.4 us  [shards(): pl.pallas_call(kernel, out_shape=(field, field), in_specs=[hbm] * 9, out_...]
    add x1 -> x0, other arithmetic: 2.53 us -> none  [shards(): return (adjoint + correction, residual - image)]
    sub x1 -> x0, other arithmetic: 1.13 us -> none  [shards(): return (adjoint + correction, residual - image)]
where the time goes in v3:
time: 80.5 us; the launch traced here: 80.4 us
  Pallas kernels  76.4 us (95%)
  local copies, waits for them, and re-layouts  3.37 us (4%)
    pallas_call x1, Pallas kernels, shards(): pl.pallas_call(kernel, out_shape=(field, field), in_specs=[hbm] * 9, out_...  76.4 us
    unnamed x4, local copies, waits for them, and re-layouts  3.37 us

profile of v3, /device:TPU:1, one launch (start us, length us, event | category | flops | bytes accessed | tf_op | source)
XLA Modules:
  0.0 80.4 jit_solution(13906123448838004951)
XLA Ops:
  0.6 76.4 %shard_map.104 = (f32[1024,256]{1,0:T(8,128)}, f32[1024,256]{1,0:T(8,128)}) custom-call(f32[256,256]{1,0:T(8,128)} %bz_hbm.1, f32[1024,256]{1,0:T(8,128)} %bitcast.9, f32[1,512]{1,0:T(1,128)} %bitcast.11, f32[1,512]{1,0:T(1,128)} %bitcast.12, f32[1,256]{1,0:T(1,128)} %bitcast.13, f32[512,512]{1,0:T(8,128)} %bx_hbm.1, f32[512,512]{1,0:T(8,128)} %by_hbm.1, ...), custom_call_target="tpu_custom_call" | custom-call | tf_op jit(solution)/shard_map/pallas_call | solution.py:443
  77.1 0.0 copy-start
  77.1 2.4 %copy.13 = f32[32,32,256]{2,1,0:T(8,128)} copy(f32[32,32,256]{2,1,0:T(8,128)} %bitcast.8) | data formatting | bytes 2097152
  79.5 0.0 copy-done
  79.5 1.0 %copy.14 = f32[32,32,256]{2,1,0:T(8,128)} copy(f32[32,32,256]{2,1,0:T(8,128)S(1)} %bitcast.7) | data formatting | bytes 2097152
Async XLA Ops:
  77.1 2.4 %copy-start = (f32[1024,256]{1,0:T(8,128)S(1)}, f32[1024,256]{1,0:T(8,128)}, u32[]{:S(2)}) copy-start(f32[1024,256]{1,0:T(8,128)} %get-tuple-element.5) | copy-start | bytes 3145732

commit v4 on v3

--- a/solution.py
+++ b/solution.py
@@ -116,8 +116,6 @@
         at = pl.ds(256 * t, 256)
         lh[at, :], ll[at, :] = split(jnp.concatenate([fbuf[0, at, :], fbuf[1, at, :]], axis=1))
 
-    prepare(0)
-
     def exchange(stage, k, src, dst, over_row):
         mine = r if over_row else n
 
@@ -154,20 +152,21 @@
         )
         send_c[k] = jnp.where(top16, a.reshape(N, 8, 512), b.reshape(N, 8, 512))
 
+    dh[1], dl[1] = split(jnp.concatenate([res[0], res[1]], axis=1))
+    prepare(1)
+    stage_z(1, 2)
+    pl.semaphore_wait(barrier, 2 * (N - 1) + 4)
+    exchange(0, 2, send_c, recv_c, False)
     for y in range(32):
         plane = jnp.concatenate([res[h, pl.ds(y, 32, stride=32), :] for h in range(2)], axis=1)
         dh[0, 32 * y : 32 * y + 32, :], dl[0, 32 * y : 32 * y + 32, :] = split(plane)
+    prepare(0)
     stage_z(0, 0)
-    pl.semaphore_wait(barrier, 2 * (N - 1) + 4)
     exchange(0, 0, send_c, recv_c, True)
-    prepare(1)
-    dh[1], dl[1] = split(jnp.concatenate([res[0], res[1]], axis=1))
-    stage_z(1, 2)
-    exchange(0, 2, send_c, recv_c, False)
+    stage_z(1, 3)
+    exchange(0, 3, send_c, recv_c, False)
     stage_z(0, 1)
     exchange(0, 1, send_c, recv_c, True)
-    stage_z(1, 3)
-    exchange(0, 3, send_c, recv_c, False)
 
     loads[3].wait()
     loads[4].wait()
@@ -249,6 +248,14 @@
                 acc[t, w, at, :] = acc[t, w, at, :] + part[:, 256 * h + 128 * w : 256 * h + 128 * w + 128]
 
     acc[...] = jnp.zeros((2, 2, 1024, 128), F32)
+    loads[8].wait()
+    for x in range(32):
+        for h in range(2):
+            wext[h, ROWS * (x + 3) + 8 : ROWS * (x + 3) + 40, :] = coef[x, :, 128 * h : 128 * h + 128].astype(F32)
+    for side, edge in ((0, 0), (1, 29)):
+        for d in range(3):
+            for h in range(2):
+                ypack[side, d, h] = wext[h, pl.ds(3 * ROWS + 8 + edge + d, 32, stride=ROWS), :]
     for x in range(38):
         for h in range(2):
             wext[h, ROWS * x : ROWS * x + 8, :] = jnp.zeros((8, 128), F32)
@@ -268,12 +275,18 @@
     pairs((first_back, 1))
     pairs((last, 1), (last, 0))
 
-    loads[8].wait()
-
     def weigh(x):
         for h in range(2):
             c = acc[0, h, pl.ds(x, 32, stride=32), :] + acc[1, h, 32 * x : 32 * x + 32, :]
-            wext[h, pl.ds(ROWS * (x + 3) + 8, 32), :] = coef[x, :, 128 * h : 128 * h + 128].astype(F32) * c
+            at = slice(ROWS * (x + 3) + 8, ROWS * (x + 3) + 40)
+            wext[h, at, :] = wext[h, at, :] * c
+
+    for side, edge in ((0, 0), (1, 29)):
+        for d in range(3):
+            for h in range(2):
+                y = edge + d
+                c = acc[0, h, 32 * y : 32 * y + 32, :] + acc[1, h, pl.ds(y, 32, stride=32), :]
+                ypack[side, d, h] = ypack[side, d, h] * c
 
     has = {(0, 0): None}
     for dr in (-1, 0, 1):
@@ -292,7 +305,8 @@
                 out.append((wext.at[:, src, :], wext.at[:, dst, :], (0 if dr < 0 else 3) + d))
         elif dr == 0:
             side = 0 if dn < 0 else 1
-            out.append((ypack.at[side], hext.at[1 - side, :, :, pl.ds(8, 32), :], 6 + side))
+            for d in range(3):
+                out.append((ypack.at[side, d], hext.at[1 - side, d, :, pl.ds(8, 32), :], 6 + 3 * side + d))
         else:
             side = 0 if dn < 0 else 1
             rows, at = (0, 40) if dr < 0 else (24, 0)
@@ -300,7 +314,7 @@
                 (
                     ypack.at[side, :, :, pl.ds(rows, 8), :],
                     hext.at[1 - side, :, :, pl.ds(at, 8), :],
-                    8 + 2 * (dr > 0) + side,
+                    12 + 2 * (dr > 0) + side,
                 )
             )
         return [
@@ -320,14 +334,12 @@
                 for c in copies(dr, dn):
                     c.start()
 
-    for x in range(32):
+    send([d for d in sides if d[0] == 0])
+    for x in (0, 1, 2, 29, 30, 31):
         weigh(x)
-    for side, first in ((0, 8), (1, 37)):
-        for d in range(3):
-            for h in range(2):
-                ypack[side, d, h] = wext[h, pl.ds(3 * ROWS + first + d, 32, stride=ROWS), :]
-    send([d for d in sides if d[0] == 0])
     send([d for d in sides if d[0] != 0])
+    for x in range(3, 29):
+        weigh(x)
 
     for dr in (-1, 1):
 
@@ -351,15 +363,6 @@
                 at = 0 if dr < 0 else 40
                 hext[0 if dn < 0 else 1, :, :, at : at + 8, :] = jnp.zeros((3, 2, 8, 128), F32)
 
-    loads[9].wait()
-    for x in range(32):
-        for h in range(2):
-            c = acc[0, h, pl.ds(x, 32, stride=32), :] + acc[1, h, 32 * x : 32 * x + 32, :]
-            at = slice(128 * h, 128 * h + 128)
-            adj[32 * x : 32 * x + 32, at] = adj[32 * x : 32 * x + 32, at] + c
-    stores = [pltpu.make_async_copy(adj, adj_out, out_sem.at[0])]
-    stores[0].start()
-
     def receive(some):
         for dr, dn in some:
 
@@ -367,8 +370,6 @@
             def _():
                 for c in copies(-dr, -dn):
                     c.wait_recv()
-
-    receive([d for d in sides if d[1] == 0])
 
     def along_rows(v):
         return [v[8:40]] + [pltpu.roll(v, d, 0)[8:40] + pltpu.roll(v, ROWS - d, 0)[8:40] for d in range(1, 4)]
@@ -386,12 +387,28 @@
             mixed[at, 256 + 128 * h : 256 + 128 * h + 128] = taps(MASS, 1.0 / 5040, mass)
         return 0
 
-    lax.fori_loop(0, 32, stencil, 0)
-    for i in range(4):
+    def finish(i):
         at = slice(256 * i, 256 * i + 256)
         image = dot3(split(mixed[at, :]), (zh[...], zl[...]))
         for h in range(2):
             res[h, at, :] = res[h, at, :] - image[:, 128 * h : 128 * h + 128]
+
+    lax.fori_loop(3, 29, stencil, 0)
+    finish(1)
+    finish(2)
+    loads[9].wait()
+    for x in range(32):
+        for h in range(2):
+            c = acc[0, h, pl.ds(x, 32, stride=32), :] + acc[1, h, 32 * x : 32 * x + 32, :]
+            at = slice(128 * h, 128 * h + 128)
+            adj[32 * x : 32 * x + 32, at] = adj[32 * x : 32 * x + 32, at] + c
+    stores = [pltpu.make_async_copy(adj, adj_out, out_sem.at[0])]
+    stores[0].start()
+    receive([d for d in sides if d[1] == 0])
+    lax.fori_loop(0, 3, stencil, 0)
+    finish(0)
+    lax.fori_loop(29, 32, stencil, 0)
+    finish(3)
 
     receive([d for d in sides if d[1] != 0])
     for side in range(2):
@@ -476,8 +493,8 @@
             pltpu.SemaphoreType.DMA((3,)),
             pltpu.SemaphoreType.DMA((4, Q)),
             pltpu.SemaphoreType.DMA((4, Q)),
-            pltpu.SemaphoreType.DMA((12,)),
-            pltpu.SemaphoreType.DMA((12,)),
+            pltpu.SemaphoreType.DMA((16,)),
+            pltpu.SemaphoreType.DMA((16,)),
         ],
         compiler_params=pltpu.CompilerParams(
             collective_id=0, has_side_effects=True, vmem_limit_bytes=56 * 1024 * 1024

time: 80.5 us -> 77.1 us (0.958)
  Pallas kernels: 76.4 us -> 72.9 us
    pallas_call x1, Pallas kernels: 76.4 us -> 72.9 us  [shards(): pl.pallas_call(kernel, out_shape=(field, field), in_specs=[hbm] * 9, out_...]
where the time goes in v4:
time: 77.1 us; the launch traced here: 76.9 us
  Pallas kernels  72.9 us (95%)
  local copies, waits for them, and re-layouts  3.37 us (4%)
    pallas_call x1, Pallas kernels, shards(): pl.pallas_call(kernel, out_shape=(field, field), in_specs=[hbm] * 9, out_...  72.9 us
    unnamed x4, local copies, waits for them, and re-layouts  3.37 us

profile of v4, /device:TPU:1, one launch (start us, length us, event | category | flops | bytes accessed | tf_op | source)
XLA Modules:
  0.0 76.9 jit_solution(12591547057808344015)
XLA Ops:
  0.6 72.9 %shard_map.104 = (f32[1024,256]{1,0:T(8,128)}, f32[1024,256]{1,0:T(8,128)}) custom-call(f32[256,256]{1,0:T(8,128)} %bz_hbm.1, f32[1024,256]{1,0:T(8,128)} %bitcast.9, f32[1,512]{1,0:T(1,128)} %bitcast.11, f32[1,512]{1,0:T(1,128)} %bitcast.12, f32[1,256]{1,0:T(1,128)} %bitcast.13, f32[512,512]{1,0:T(8,128)} %bx_hbm.1, f32[512,512]{1,0:T(8,128)} %by_hbm.1, ...), custom_call_target="tpu_custom_call" | custom-call | tf_op jit(solution)/shard_map/pallas_call | solution.py:460
  73.5 0.0 copy-start
  73.6 2.4 %copy.13 = f32[32,32,256]{2,1,0:T(8,128)} copy(f32[32,32,256]{2,1,0:T(8,128)} %bitcast.8) | data formatting | bytes 2097152
  75.9 0.0 copy-done
  76.0 1.0 %copy.14 = f32[32,32,256]{2,1,0:T(8,128)} copy(f32[32,32,256]{2,1,0:T(8,128)S(1)} %bitcast.7) | data formatting | bytes 2097152
Async XLA Ops:
  73.5 2.4 %copy-start = (f32[1024,256]{1,0:T(8,128)S(1)}, f32[1024,256]{1,0:T(8,128)}, u32[]{:S(2)}) copy-start(f32[1024,256]{1,0:T(8,128)} %get-tuple-element.5) | copy-start | bytes 3145732

commit v5 on v4

--- a/solution.py
+++ b/solution.py
@@ -78,7 +78,7 @@
         pltpu.make_async_copy(src, dst, in_sem.at[s])
         for s, (src, dst) in enumerate(
             (
-                (bz_hbm, bz), (res_hbm.at[:, :128], res.at[0]), (res_hbm.at[:, 128:], res.at[1]),
+                (bz_hbm, bz), (res_hbm.at[:, :128], res.at[0, :1024]), (res_hbm.at[:, 128:], res.at[1, :1024]),
                 (bx_hbm, bx), (by_hbm, by), (ex_hbm, ex), (ey_hbm, ey), (ez_hbm, ez), (coef_hbm, coef),
                 (adj_hbm, adj),
             )
@@ -152,7 +152,7 @@
         )
         send_c[k] = jnp.where(top16, a.reshape(N, 8, 512), b.reshape(N, 8, 512))
 
-    dh[1], dl[1] = split(jnp.concatenate([res[0], res[1]], axis=1))
+    dh[1], dl[1] = split(jnp.concatenate([res[0, :1024], res[1, :1024]], axis=1))
     prepare(1)
     stage_z(1, 2)
     pl.semaphore_wait(barrier, 2 * (N - 1) + 4)
@@ -247,7 +247,7 @@
                 at = pl.ds(512 * h, 512)
                 acc[t, w, at, :] = acc[t, w, at, :] + part[:, 256 * h + 128 * w : 256 * h + 128 * w + 128]
 
-    acc[...] = jnp.zeros((2, 2, 1024, 128), F32)
+    acc[...] = jnp.zeros((2, 2, 1056, 128), F32)
     loads[8].wait()
     for x in range(32):
         for h in range(2):
@@ -271,8 +271,7 @@
 
     pairs((first, 1), (first, 0))
     pairs((middle, 0), (middle, 1))
-    pairs((first_back, 0))
-    pairs((first_back, 1))
+    pairs((first_back, 0), (first_back, 1))
     pairs((last, 1), (last, 0))
 
     def weigh(x):
@@ -432,7 +431,7 @@
                 at = pl.ds(o if side == 0 else 29 + o, 32, stride=32)
                 part = image[96 * side + 32 * o : 96 * side + 32 * o + 32, 128 * h : 128 * h + 128]
                 res[h, at, :] = res[h, at, :] - part
-        store = pltpu.make_async_copy(res.at[h], res_out.at[:, pl.ds(128 * h, 128)], out_sem.at[1 + h])
+        store = pltpu.make_async_copy(res.at[h, :1024], res_out.at[:, pl.ds(128 * h, 128)], out_sem.at[1 + h])
         store.start()
         stores.append(store)
 
@@ -464,7 +463,7 @@
         out_specs=(hbm, hbm),
         scratch_shapes=[
             pltpu.VMEM((256, 256), F32),
-            pltpu.VMEM((2, 1024, 128), F32),
+            pltpu.VMEM((2, 1056, 128), F32),
             pltpu.VMEM((1, 512), F32),
             pltpu.VMEM((1, 512), F32),
             pltpu.VMEM((1, 256), F32),
@@ -484,7 +483,7 @@
             wide, wide, tall, tall, tall, tall, wide, wide,
             pltpu.VMEM((4, 512, 128), F32),
             pltpu.VMEM((128, 512), F32),
-            pltpu.VMEM((2, 2, 1024, 128), F32),
+            pltpu.VMEM((2, 2, 1056, 128), F32),
             pltpu.VMEM((2, 38 * ROWS, 128), F32),
             pltpu.VMEM((2, 3, 2, 32, 128), F32),
             pltpu.VMEM((2, 3, 2, ROWS, 128), F32),

time: 77.1 us -> 77 us (level)
  Pallas kernels: 72.9 us -> 72.1 us
    pallas_call x1, Pallas kernels: 72.9 us -> 72.1 us  [shards(): pl.pallas_call(kernel, out_shape=(field, field), in_specs=[hbm] * 9, out_...]
where the time goes in v5:
time: 77 us; the launch traced here: 76.1 us
  Pallas kernels  72.1 us (94%)
  local copies, waits for them, and re-layouts  3.37 us (4%)
    pallas_call x1, Pallas kernels, shards(): pl.pallas_call(kernel, out_shape=(field, field), in_specs=[hbm] * 9, out_...  72.1 us
    unnamed x4, local copies, waits for them, and re-layouts  3.37 us

profile of v5, /device:TPU:1, one launch (start us, length us, event | category | flops | bytes accessed | tf_op | source)
XLA Modules:
  0.0 76.1 jit_solution(7966304383779392887)
XLA Ops:
  0.6 72.1 %shard_map.104 = (f32[1024,256]{1,0:T(8,128)}, f32[1024,256]{1,0:T(8,128)}) custom-call(f32[256,256]{1,0:T(8,128)} %bz_hbm.1, f32[1024,256]{1,0:T(8,128)} %bitcast.9, f32[1,512]{1,0:T(1,128)} %bitcast.11, f32[1,512]{1,0:T(1,128)} %bitcast.12, f32[1,256]{1,0:T(1,128)} %bitcast.13, f32[512,512]{1,0:T(8,128)} %bx_hbm.1, f32[512,512]{1,0:T(8,128)} %by_hbm.1, ...), custom_call_target="tpu_custom_call" | custom-call | tf_op jit(solution)/shard_map/pallas_call | solution.py:459
  72.7 0.0 copy-start
  72.7 2.4 %copy.13 = f32[32,32,256]{2,1,0:T(8,128)} copy(f32[32,32,256]{2,1,0:T(8,128)} %bitcast.8) | data formatting | bytes 2097152
  75.1 0.0 copy-done
  75.1 1.0 %copy.14 = f32[32,32,256]{2,1,0:T(8,128)} copy(f32[32,32,256]{2,1,0:T(8,128)S(1)} %bitcast.7) | data formatting | bytes 2097152
Async XLA Ops:
  72.7 2.4 %copy-start = (f32[1024,256]{1,0:T(8,128)S(1)}, f32[1024,256]{1,0:T(8,128)}, u32[]{:S(2)}) copy-start(f32[1024,256]{1,0:T(8,128)} %get-tuple-element.5) | copy-start | bytes 3145732
